TPU v7x, 128 devices: a whole 4x4x4 slice. The times are simulated.
128 devices in a mesh: branch: 4 (over z), ctx: 32 (over y, x, core).
Axes of the slice: x: 4, y: 4, z: 4, core: 2. Of those that a mesh axis runs over, the one named last changes fastest.
Arguments:
- summary_q: bfloat16 [65536, 2560], P(('branch', 'ctx')), may hold values from -32 to 32
- summary_kv: bfloat16 [65536, 2, 512], P(('branch', 'ctx')), may hold values from -12 to 12
- kv_cache: bfloat16 [512, 2, 128, 512], P(('branch', 'ctx')), may hold values from -9 to 9
- block_slot: int32 [512], replicated, may hold values from 0 to 511, as said below
- tile_blocks: int32 [512, 8], P(('branch', 'ctx')), may hold values from 0 to 511, as said below
- tile_count: int32 [512], P(('branch', 'ctx')), may hold values from 2 to 8
Outputs:
- attended: bfloat16 [65536, 2560], P(('branch', 'ctx'))
Inputs may be any that keep to these rules, and one draw needn't show every extreme that they name: `block_slot`: each slot number appears once; slot s lies on the device of index s // 4 along branch+ctx. `tile_blocks`: among the first tile_count[t] entries of the 4 tiles of one device, at most 2 are stored on devices of one ctx index and at most 1 on one device; entries after tile_count[t] are not read.
All inputs are finite; a program needn't handle non-finite values.
Results may differ from a plain program's by a relative error of at most 0.0045.
Values may be sent and summed in bfloat16 or wider, within the bound.
No kernel may reach another device: no remote copies, remote signals or barrier semaphores. Data moves between devices by JAX's collectives and lax.ppermute only.
A program may use at most 192 MiB of HBM per device.

v0:
```python
import jax
import jax.numpy as jnp
from jax import lax
from jax.sharding import PartitionSpec as P

HEAD = 128
REQ_TILES = 32


def from_behind(value, axis, steps):
    count = lax.axis_size(axis)
    pairs = [(source, (source + steps) % count) for source in range(count)]
    return lax.ppermute(value, axis, pairs)


def request_table(dest_index, live_mask, count_dest, capacity, payload):
    onehot = (
        (dest_index[:, None] == jnp.arange(count_dest, dtype=jnp.int32)[None, :])
        & live_mask[:, None]
    ).astype(jnp.int32)
    rank_within = jnp.sum(onehot * (jnp.cumsum(onehot, axis=0) - 1), axis=1)
    position = dest_index * capacity + rank_within
    target = jnp.where(live_mask, position, -1)
    slot_ids = jnp.arange(count_dest * capacity, dtype=jnp.int32)
    requests = jnp.max(
        jnp.where(target[:, None] == slot_ids[None, :], payload[:, None], -1), axis=0
    )
    return (requests.reshape(count_dest, capacity), position)


def absorb(running, queries, key_rows, value_rows, key_mask, score_form, value_form, score_scale):
    old_max, old_sum, old_weighted = running
    block_scores = (
        jnp.einsum(score_form, queries, key_rows, preferred_element_type=jnp.float32) * score_scale
    )
    if key_mask is not None:
        block_scores = jnp.where(key_mask, block_scores, -jnp.inf)
    new_max = jnp.maximum(old_max, jnp.max(block_scores, axis=-1))
    block_weights = jnp.exp(block_scores - new_max[..., None])
    rescale = jnp.exp(old_max - new_max)
    new_sum = old_sum * rescale + jnp.sum(block_weights, axis=-1)
    new_weighted = old_weighted * rescale[..., None] + jnp.einsum(
        value_form,
        block_weights.astype(jnp.bfloat16),
        value_rows,
        preferred_element_type=jnp.float32,
    )
    return (new_max, new_sum, new_weighted)


def keep_state(running, earlier):
    return running


def local(summary_q, summary_kv, kv_cache, block_slot, tile_blocks, tile_count):
    shards = lax.axis_size("ctx")
    tile_num, list_len = tile_blocks.shape
    blk_dev = kv_cache.shape[0]
    block_len = kv_cache.shape[2]
    kv_width = kv_cache.shape[3]
    kv_heads = kv_width // HEAD
    rows = summary_q.shape[0]
    tile_rows = rows // tile_num
    repeat = summary_q.shape[1] // kv_width
    col_cap = max(2, -(-(tile_num * list_len) // shards))
    req_devs = REQ_TILES // tile_num
    score_scale = HEAD ** (-0.5)
    entries = tile_blocks.reshape(-1)
    live_mask = (jnp.arange(list_len, dtype=jnp.int32)[None, :] < tile_count[:, None]).reshape(-1)
    block_ids = jnp.arange(block_slot.shape[0], dtype=jnp.int32)
    stored_at = jnp.sum(
        jnp.where(entries[:, None] == block_ids[None, :], block_slot[None, :], 0), axis=1
    )
    owner_dev = stored_at // blk_dev
    local_slot = stored_at % blk_dev
    column = lax.all_gather(kv_cache, "branch", axis=0, tiled=True)
    requests, position = request_table(
        owner_dev % shards, live_mask, shards, col_cap, owner_dev // shards * blk_dev + local_slot
    )
    payload = column[
        jnp.maximum(lax.all_to_all(requests, "ctx", split_axis=0, concat_axis=0, tiled=True), 0)
    ]
    received = lax.all_to_all(payload, "ctx", split_axis=0, concat_axis=0, tiled=True)
    received = received.reshape(-1, 2, block_len, kv_width)
    position = jnp.where(live_mask, position, 0).reshape(tile_num, list_len)
    queries = summary_q.reshape(tile_num, tile_rows, kv_heads, repeat, HEAD)
    own_kv = summary_kv.reshape(rows, 2, kv_heads, HEAD)
    query_pos = jnp.arange(rows, dtype=jnp.int32).reshape(tile_num, tile_rows)
    causal = (
        query_pos[:, None, None, :, None]
        >= jnp.arange(rows, dtype=jnp.int32)[None, None, None, None, :]
    )
    scores = (
        jnp.einsum("tqgrd,kgd->tgrqk", queries, own_kv[:, 0], preferred_element_type=jnp.float32)
        * score_scale
    )
    scores = jnp.where(causal, scores, -jnp.inf)
    row_max = jnp.max(scores, axis=-1)
    weights = jnp.exp(scores - row_max[..., None])
    row_sum = jnp.sum(weights, axis=-1)
    weighted = jnp.einsum(
        "tgrqk,kgd->tgrqd",
        weights.astype(jnp.bfloat16),
        own_kv[:, 1],
        preferred_element_type=jnp.float32,
    )
    running = (row_max, row_sum, weighted)

    def take_earlier(state, earlier):
        return absorb(
            state,
            queries,
            earlier[:, 0],
            earlier[:, 1],
            None,
            "tqgrd,kgd->tgrqk",
            "tgrqk,kgd->tgrqd",
            score_scale,
        )

    flat_index = lax.axis_index("branch") * shards + lax.axis_index("ctx")
    place = (flat_index - 1 + req_devs) % req_devs
    for distance in range(1, req_devs):
        earlier = from_behind(summary_kv, ("branch", "ctx"), distance)
        running = lax.cond(
            place >= distance,
            take_earlier,
            keep_state,
            running,
            earlier.reshape(rows, 2, kv_heads, HEAD),
        )
    pair_slots = position.reshape(tile_num, list_len // 2, 2)
    step_count = (jnp.max(tile_count) + 1) // 2

    def advance(step_idx, state):
        where_now = lax.dynamic_index_in_dim(pair_slots, step_idx, axis=1, keepdims=False)
        blocks = received[where_now]
        key_rows = blocks[:, :, 0].reshape(tile_num, 2 * block_len, kv_heads, HEAD)
        value_rows = blocks[:, :, 1].reshape(tile_num, 2 * block_len, kv_heads, HEAD)
        valid_keys = (step_idx * 2 + jnp.arange(2, dtype=jnp.int32))[None, :] < tile_count[:, None]
        valid_keys = jnp.repeat(valid_keys, block_len, axis=1)
        return absorb(
            state,
            queries,
            key_rows,
            value_rows,
            valid_keys[:, None, None, None, :],
            "tqgrd,tkgd->tgrqk",
            "tgrqk,tkgd->tgrqd",
            score_scale,
        )

    row_max, row_sum, weighted = lax.fori_loop(0, step_count, advance, running)
    result = (
        (weighted / row_sum[..., None]).transpose(0, 3, 1, 2, 4).reshape(tile_num * tile_rows, -1)
    )
    return result.astype(jnp.bfloat16)


def solution(mesh):
    in_specs = (
        P(("branch", "ctx"), None),
        P(("branch", "ctx"), None, None),
        P(("branch", "ctx"), None, None, None),
        P(),
        P(("branch", "ctx"), None),
        P(("branch", "ctx")),
    )
    out_specs = P(("branch", "ctx"), None)
    return jax.shard_map(local, mesh=mesh, in_specs=in_specs, out_specs=out_specs, check_vma=False)
```

profile of v0, /device:TPU:8, one launch (start us, length us, event | category | flops | bytes accessed | tf_op | source)
XLA Modules:
  0.0 669.2 jit_solution(16683268028357404314)
XLA Ops:
  10.3 13.5 %all_to_all.14 = s32[32,1,2]{2,1,0:T(1,128)S(1)} all-to-all(s32[32,1,2]{2,1,0:T(1,128)S(1)} %bitcast.316), channel_id=1, replica_groups=mesh['branch'=4,'ctx'=32] {'ctx'}, dimensions={0} | all-to-all | bytes 512 | tf_op jit(solution)/shard_map/all_to_all | solution.py:81
  24.0 35.7 %all-gather.2.cloned.1.call-done = bf16[16,2,128,512]{3,2,1,0:T(8,128)(2,1)} async-done(((bf16[4,2,128,512]{3,2,1,0:T(8,128)(2,1)}), bf16[16,2,128,512]{3,2,1,0:T(8,128)(2,1)}) %all-gather.2.cloned.1.call-update) | async-done | bytes 4194320 | tf_op jit(solution)/shard_map/all_gather | solution.py:76
  59.7 9.6 %gather_fusion.1 = bf16[64,2,128,512]{3,2,1,0:T(8,128)(2,1)} fusion(bf16[16,2,128,512]{3,2,1,0:T(8,128)(2,1)} %all-gather.2.cloned.1.call-done, s32[1024]{0:T(1024)S(1)} %pad_clamp_fusion.1), kind=kCustom, calls=%fused_computation.1 | custom fusion | bytes 33554688 | tf_op jit(solution)/shard_map/gather | solution.py:80
  69.4 7.9 %all-to-all-start.1 = ((bf16[32,2,2,128,512]{4,3,2,1,0:T(8,128)(2,1)}), bf16[32,2,2,128,512]{4,3,2,1,0:T(8,128)(2,1)}, u32[]{:S(2)}, u32[]{:S(2)}) async-start(bf16[32,2,2,128,512]{4,3,2,1,0:T(8,128)(2,1)} %bitcast.315), calls=%async_computation.1 | async-start | bytes 33554432 | tf_op jit(solution)/shard_map/all_to_all | solution.py:83
  101.1 9.8 %fusion.102 = (f32[4,4,5,128]{3,2,0,1:T(8,128)S(1)}, f32[4,512,4,128,5]{3,1,4,2,0:T(8,128)}) fusion(pred[4,128,512]{1,2,0:T(8,128)(4,1)S(1)} %iota_compare_fusion, bf16[4,128,4,5,128]{1,0,4,3,2:T(4,128)(2,1)S(1)} %reshape.233, bf16[512,2,4,128]{0,3,2,1:T(8,128)(2,1)} %bitcast.63), kind=kOutput, calls=%fused_computation.144 | convolution fusion | flops 1357895680 | bytes 24420352 | tf_op jit(solution)/shard_map/tqgrd,kgd->tgrqk/dot_general | solution.py:94
  110.9 11.5 %fusion.109 = f32[4,4,5,128,128]{4,3,2,0,1:T(8,128)} fusion(f32[4,512,4,128,5]{3,1,4,2,0:T(8,128)} %get-tuple-element.483, f32[4,4,5,128]{3,2,0,1:T(8,128)S(1)} %get-tuple-element.482, pred[4,128,512]{1,2,0:T(8,128)(4,1)S(1)} %iota_compare_fusion, bf16[512,2,4,128]{0,3,2,1:T(8,128)(2,1)} %bitcast.63), kind=kOutput, calls=%fused_computation.151 | convolution fusion | flops 1363148800 | bytes 27041792 | tf_op jit(solution)/shard_map/tgrqk,kgd->tgrqd/dot_general | solution.py:101
  122.4 168.8 %collective-permute-done = bf16[512,2,512]{0,2,1:T(8,128)(2,1)} collective-permute-done((bf16[512,2,512]{0,2,1:T(8,128)(2,1)}, bf16[512,2,512]{0,2,1:T(8,128)(2,1)}, u32[]{:S(2)}, u32[]{:S(2)}) %collective-permute-start) | collective-permute-done | bytes 1048608 | tf_op jit(solution)/shard_map/ppermute | solution.py:13
  291.2 20.1 %collective-permute-start.5 = (bf16[512,2,512]{0,2,1:T(8,128)(2,1)}, bf16[512,2,512]{0,2,1:T(8,128)(2,1)}, u32[]{:S(2)}, u32[]{:S(2)}) collective-permute-start(bf16[512,2,512]{0,2,1:T(8,128)(2,1)} %copy.142), channel_id=1, source_target_pairs={{0,6},{1,7},{2,8},{3,9},{4,10},{5,11},{6,12},{7,13},{8,14},{9,15},... | collective-permute-start | bytes 3145736 | tf_op jit(solution)/shard_map/ppermute | solution.py:13
  311.3 22.7 %collective-permute-start.6 = (bf16[512,2,512]{0,2,1:T(8,128)(2,1)}, bf16[512,2,512]{0,2,1:T(8,128)(2,1)}, u32[]{:S(2)}, u32[]{:S(2)}) collective-permute-start(bf16[512,2,512]{0,2,1:T(8,128)(2,1)} %copy.142), channel_id=1, source_target_pairs={{0,7},{1,8},{2,9},{3,10},{4,11},{5,12},{6,13},{7,14},{8,15},{9,16}... | collective-permute-start | bytes 3145736 | tf_op jit(solution)/shard_map/ppermute | solution.py:13
  334.0 9.5 %fusion.101 = f32[4,4,5,128]{3,2,0,1:T(8,128)S(1)} fusion(f32[4,512,4,128,5]{3,1,4,2,0:T(8,128)} %get-tuple-element.483, f32[4,4,5,128]{3,2,0,1:T(8,128)S(1)} %get-tuple-element.482, pred[4,128,512]{1,2,0:T(8,128)(4,1)S(1)} %iota_compare_fusion), kind=kLoop, calls=%fused_computation.143 | loop fusion | flops 20961280 | bytes 21315584 | tf_op jit(solution)/shard_map/reduce_sum | solution.py:100
  343.5 26.4 %conditional.7 = ((f32[4,4,5,128]{3,2,0,1:T(8,128)S(1)}, f32[4,4,5,128]{3,2,0,1:T(8,128)S(1)}, f32[4,4,5,128,128]{4,3,2,0,1:T(8,128)})) conditional(s32[]{:T(128)} %convert_element_type.66, (f32[4,4,5,128]{3,2,0,1:T(8,128)S(1)}, f32[4,4,5,128]{3,2,0,1:T(8,128)S(1)}, f32[4,4,5,128,128]{4,3,2,0,1:T(8,128)}) %tuple.52, ...), branch_computations={%region_2.3_spmd, %region_3.6_spmd} | conditional | flops 2728939520 | bytes 167952480 | solution.py:125
  357.1 12.8 %bitcast_add_fusion = f32[4,4,5,128,128]{4,3,2,0,1:T(8,128)} fusion(f32[4,4,5,128,128]{4,3,2,0,1:T(8,128)} %get-tuple-element.158, f32[4,4,5,128]{3,2,0,1:T(8,128)S(1)} %get-tuple-element.447, f32[4,512,4,128,5]{3,1,4,2,0:T(8,128)} %copy-done.1, f32[4,4,5,128]{3,2,0,1:T(8,128)S(1)} %max.27, bf16[512,2,4,128]{3,0,2,1:T(8,128)(2,1)S(1)} %copy-done.8), kind=kOutput, calls=%fused_computation.10 | convolution fusion | flops 1360527360 | bytes 32112640 | tf_op jit(solution)/shard_map/cond/branch_1_fun/tgrqk,kgd->tgrqd/dot_general | solution.py:42
  370.0 26.6 %conditional.8 = ((f32[4,4,5,128]{3,2,0,1:T(8,128)S(1)}, f32[4,4,5,128]{3,2,0,1:T(8,128)S(1)}, f32[4,4,5,128,128]{4,3,2,0,1:T(8,128)})) conditional(s32[]{:T(128)} %convert_element_type.65, (f32[4,4,5,128]{3,2,0,1:T(8,128)S(1)}, f32[4,4,5,128]{3,2,0,1:T(8,128)S(1)}, f32[4,4,5,128,128]{4,3,2,0,1:T(8,128)}) %get-tuple-element.633, ...), branch_computations={%region_6.7_spmd, %region_7.10_spmd} | conditional | flops 2728939520 | bytes 167952480 | solution.py:125
  383.8 12.8 %bitcast_add_fusion.1 = f32[4,4,5,128,128]{4,3,2,0,1:T(8,128)} fusion(f32[4,4,5,128,128]{4,3,2,0,1:T(8,128)} %get-tuple-element.163, f32[4,4,5,128]{3,2,0,1:T(8,128)S(1)} %get-tuple-element.449, f32[4,512,4,128,5]{3,1,4,2,0:T(8,128)} %copy-done.2, f32[4,4,5,128]{3,2,0,1:T(8,128)S(1)} %max.28, bf16[512,2,4,128]{3,0,2,1:T(8,128)(2,1)S(1)} %copy-done.9), kind=kOutput, calls=%fused_computation.26 | convolution fusion | flops 1360527360 | bytes 32112640 | tf_op jit(solution)/shard_map/cond/branch_1_fun/tgrqk,kgd->tgrqd/dot_general | solution.py:42
  396.6 26.6 %conditional.9 = ((f32[4,4,5,128]{3,2,0,1:T(8,128)S(1)}, f32[4,4,5,128]{3,2,0,1:T(8,128)S(1)}, f32[4,4,5,128,128]{4,3,2,0,1:T(8,128)})) conditional(s32[]{:T(128)} %convert_element_type.64, (f32[4,4,5,128]{3,2,0,1:T(8,128)S(1)}, f32[4,4,5,128]{3,2,0,1:T(8,128)S(1)}, f32[4,4,5,128,128]{4,3,2,0,1:T(8,128)}) %get-tuple-element.634, ...), branch_computations={%region_10.11_spmd, %region_11.14_spmd} | conditional | flops 2728939520 | bytes 167952480 | solution.py:125
  410.4 12.8 %bitcast_add_fusion.2 = f32[4,4,5,128,128]{4,3,2,0,1:T(8,128)} fusion(f32[4,4,5,128,128]{4,3,2,0,1:T(8,128)} %get-tuple-element.168, f32[4,4,5,128]{3,2,0,1:T(8,128)S(1)} %get-tuple-element.451, f32[4,512,4,128,5]{3,1,4,2,0:T(8,128)} %copy-done.3, f32[4,4,5,128]{3,2,0,1:T(8,128)S(1)} %max.29, bf16[512,2,4,128]{3,0,2,1:T(8,128)(2,1)S(1)} %copy-done.10), kind=kOutput, calls=%fused_computation.42 | convolution fusion | flops 1360527360 | bytes 32112640 | tf_op jit(solution)/shard_map/cond/branch_1_fun/tgrqk,kgd->tgrqd/dot_general | solution.py:42
  423.3 26.7 %conditional.10 = ((f32[4,4,5,128]{3,2,0,1:T(8,128)S(1)}, f32[4,4,5,128]{3,2,0,1:T(8,128)S(1)}, f32[4,4,5,128,128]{4,3,2,0,1:T(8,128)})) conditional(s32[]{:T(128)} %convert_element_type.63, (f32[4,4,5,128]{3,2,0,1:T(8,128)S(1)}, f32[4,4,5,128]{3,2,0,1:T(8,128)S(1)}, f32[4,4,5,128,128]{4,3,2,0,1:T(8,128)}) %get-tuple-element.635, ...), branch_computations={%region_14.15_spmd, %region_15.18_spmd} | conditional | flops 2728939520 | bytes 167952480 | solution.py:125
  437.1 12.8 %bitcast_add_fusion.3 = f32[4,4,5,128,128]{4,3,2,0,1:T(8,128)} fusion(f32[4,4,5,128,128]{4,3,2,0,1:T(8,128)} %get-tuple-element.173, f32[4,4,5,128]{3,2,0,1:T(8,128)S(1)} %get-tuple-element.453, f32[4,512,4,128,5]{3,1,4,2,0:T(8,128)} %copy-done.4, f32[4,4,5,128]{3,2,0,1:T(8,128)S(1)} %max.30, bf16[512,2,4,128]{3,0,2,1:T(8,128)(2,1)S(1)} %copy-done.11), kind=kOutput, calls=%fused_computation.58 | convolution fusion | flops 1360527360 | bytes 32112640 | tf_op jit(solution)/shard_map/cond/branch_1_fun/tgrqk,kgd->tgrqd/dot_general | solution.py:42
  450.0 26.7 %conditional.11 = ((f32[4,4,5,128]{3,2,0,1:T(8,128)S(1)}, f32[4,4,5,128]{3,2,0,1:T(8,128)S(1)}, f32[4,4,5,128,128]{4,3,2,0,1:T(8,128)})) conditional(s32[]{:T(128)} %convert_element_type.62, (f32[4,4,5,128]{3,2,0,1:T(8,128)S(1)}, f32[4,4,5,128]{3,2,0,1:T(8,128)S(1)}, f32[4,4,5,128,128]{4,3,2,0,1:T(8,128)}) %get-tuple-element.636, ...), branch_computations={%region_18.19_spmd, %region_19.22_spmd} | conditional | flops 2728939520 | bytes 167952480 | solution.py:125
  463.9 12.8 %bitcast_add_fusion.4 = f32[4,4,5,128,128]{4,3,2,0,1:T(8,128)} fusion(f32[4,4,5,128,128]{4,3,2,0,1:T(8,128)} %get-tuple-element.178, f32[4,4,5,128]{3,2,0,1:T(8,128)S(1)} %get-tuple-element.455, f32[4,512,4,128,5]{3,1,4,2,0:T(8,128)} %copy-done.5, f32[4,4,5,128]{3,2,0,1:T(8,128)S(1)} %max.31, bf16[512,2,4,128]{3,0,2,1:T(8,128)(2,1)S(1)} %copy-done.12), kind=kOutput, calls=%fused_computation.74 | convolution fusion | flops 1360527360 | bytes 32112640 | tf_op jit(solution)/shard_map/cond/branch_1_fun/tgrqk,kgd->tgrqd/dot_general | solution.py:42
  476.7 26.9 %conditional.12 = ((f32[4,4,5,128]{3,2,0,1:T(8,128)S(1)}, f32[4,4,5,128]{3,2,0,1:T(8,128)S(1)}, f32[4,4,5,128,128]{4,3,2,0,1:T(8,128)})) conditional(s32[]{:T(128)} %convert_element_type.61, (f32[4,4,5,128]{3,2,0,1:T(8,128)S(1)}, f32[4,4,5,128]{3,2,0,1:T(8,128)S(1)}, f32[4,4,5,128,128]{4,3,2,0,1:T(8,128)}) %get-tuple-element.637, ...), branch_computations={%region_22.23_spmd, %region_23.26_spmd} | conditional | flops 2728939520 | bytes 167952480 | solution.py:125
  490.8 12.8 %bitcast_add_fusion.5 = f32[4,4,5,128,128]{4,3,2,0,1:T(8,128)} fusion(f32[4,4,5,128,128]{4,3,2,0,1:T(8,128)} %get-tuple-element.183, f32[4,4,5,128]{3,2,0,1:T(8,128)S(1)} %get-tuple-element.457, f32[4,512,4,128,5]{3,1,4,2,0:T(8,128)} %copy-done.6, f32[4,4,5,128]{3,2,0,1:T(8,128)S(1)} %max.32, bf16[512,2,4,128]{3,0,2,1:T(8,128)(2,1)S(1)} %copy-done.13), kind=kOutput, calls=%fused_computation.90 | convolution fusion | flops 1360527360 | bytes 32112640 | tf_op jit(solution)/shard_map/cond/branch_1_fun/tgrqk,kgd->tgrqd/dot_general | solution.py:42
  503.7 26.0 %conditional.13 = (f32[4,4,5,128]{3,2,1,0:T(8,128)S(1)}, f32[4,4,5,128]{3,2,1,0:T(8,128)S(1)}, f32[4,4,5,128,128]{4,3,2,1,0:T(8,128)}) conditional(s32[]{:T(128)} %convert_element_type.60, (f32[4,4,5,128]{3,2,0,1:T(8,128)S(1)}, f32[4,4,5,128]{3,2,0,1:T(8,128)S(1)}, f32[4,4,5,128,128]{4,3,2,0,1:T(8,128)}) %get-tuple-element.638, ...), branch_computations={%region_26.27_spmd, %region_27.30_spmd} | conditional | flops 2728939520 | bytes 172179520 | solution.py:125
  515.0 11.6 %bitcast_add_fusion.6 = f32[4,4,5,128,128]{4,3,2,0,1:T(8,128)S(1)} fusion(f32[4,4,5,128,128]{4,3,2,0,1:T(8,128)} %get-tuple-element.188, f32[4,4,5,128]{3,2,0,1:T(8,128)S(1)} %get-tuple-element.459, f32[4,512,4,128,5]{3,1,4,2,0:T(8,128)} %copy-done.7, f32[4,4,5,128]{3,2,0,1:T(8,128)S(1)} %max.33, bf16[512,2,4,128]{0,3,2,1:T(8,128)(2,1)} %bitcast.48), kind=kOutput, calls=%fused_computation.106 | convolution fusion | flops 1360527360 | bytes 32063488 | tf_op jit(solution)/shard_map/cond/branch_1_fun/tgrqk,kgd->tgrqd/dot_general | solution.py:42
  529.7 118.3 %while.14 = (s32[]{:T(128)}, f32[4,4,5,128]{3,2,1,0:T(8,128)S(1)}, f32[4,4,5,128]{3,2,1,0:T(8,128)S(1)}, f32[4,4,5,128,128]{4,3,2,1,0:T(8,128)}, s32[]{:T(128)},...) while((s32[]{:T(128)}, f32[4,4,5,128]{3,2,1,0:T(8,128)S(1)}, ...), condition=%wide.region_38.39_spmd, body=%wide.region_35.38_spmd.sunk | while | flops 1373656064 | bytes 101851640 | solution.py:153
  530.8 6.5 gather_fusion
  550.5 8.9 %multiply_add_fusion.14 = f32[4,4,5,128,128]{4,3,2,1,0:T(8,128)} fusion(f32[4,4,5,128,128]{4,3,2,1,0:T(8,128)} %get-tuple-element.610, f32[4,4,5,128]{3,2,1,0:T(8,128)S(1)} %get-tuple-element.550, f32[4,4,256,128,5]{3,2,4,1,0:T(8,128)} %copy-done, f32[4,4,5,128]{3,2,1,0:T(8,128)S(1)} %max.41, pred[4,256]{1,0:T(4,128)(4,1)S(1)} %broadcast_bitcast_fusion.2, ...), kind=kOutput, calls=%fused_computation.121.clone.1 | convolution fusion | flops 684195840 | bytes 22103040 | tf_op jit(solution)/shard_map/while/body/tgrqk,tkgd->tgrqd/dot_general | solution.py:42
  560.3 6.5 gather_fusion
  580.0 8.9 %multiply_add_fusion.14 = f32[4,4,5,128,128]{4,3,2,1,0:T(8,128)} fusion(f32[4,4,5,128,128]{4,3,2,1,0:T(8,128)} %get-tuple-element.610, f32[4,4,5,128]{3,2,1,0:T(8,128)S(1)} %get-tuple-element.550, f32[4,4,256,128,5]{3,2,4,1,0:T(8,128)} %copy-done, f32[4,4,5,128]{3,2,1,0:T(8,128)S(1)} %max.41, pred[4,256]{1,0:T(4,128)(4,1)S(1)} %broadcast_bitcast_fusion.2, ...), kind=kOutput, calls=%fused_computation.121.clone.1 | convolution fusion | flops 684195840 | bytes 22103040 | tf_op jit(solution)/shard_map/while/body/tgrqk,tkgd->tgrqd/dot_general | solution.py:42
  609.5 8.9 %multiply_add_fusion.14 = f32[4,4,5,128,128]{4,3,2,1,0:T(8,128)} fusion(f32[4,4,5,128,128]{4,3,2,1,0:T(8,128)} %get-tuple-element.610, f32[4,4,5,128]{3,2,1,0:T(8,128)S(1)} %get-tuple-element.550, f32[4,4,256,128,5]{3,2,4,1,0:T(8,128)} %copy-done, f32[4,4,5,128]{3,2,1,0:T(8,128)S(1)} %max.41, pred[4,256]{1,0:T(4,128)(4,1)S(1)} %broadcast_bitcast_fusion.2, ...), kind=kOutput, calls=%fused_computation.121.clone.1 | convolution fusion | flops 684195840 | bytes 22103040 | tf_op jit(solution)/shard_map/while/body/tgrqk,tkgd->tgrqd/dot_general | solution.py:42
  639.0 8.9 %multiply_add_fusion.14 = f32[4,4,5,128,128]{4,3,2,1,0:T(8,128)} fusion(f32[4,4,5,128,128]{4,3,2,1,0:T(8,128)} %get-tuple-element.610, f32[4,4,5,128]{3,2,1,0:T(8,128)S(1)} %get-tuple-element.550, f32[4,4,256,128,5]{3,2,4,1,0:T(8,128)} %copy-done, f32[4,4,5,128]{3,2,1,0:T(8,128)S(1)} %max.41, pred[4,256]{1,0:T(4,128)(4,1)S(1)} %broadcast_bitcast_fusion.2, ...), kind=kOutput, calls=%fused_computation.121.clone.1 | convolution fusion | flops 684195840 | bytes 22103040 | tf_op jit(solution)/shard_map/while/body/tgrqk,tkgd->tgrqd/dot_general | solution.py:42
  655.1 7.0 %reshape.278 = bf16[512,2560]{1,0:T(8,128)(2,1)} reshape(bf16[4,128,4,5,128]{4,3,2,1,0:T(8,128)(2,1)} %copy.207) | data formatting | bytes 5242880 | tf_op jit(solution)/shard_map/convert_element_type | solution.py:157
  (188 shorter events, 198.4 us)
Async XLA Ops:
  6.5 53.2 %all-gather.2.cloned.1.call-start = ((), (), s32[]{:S(2)}) async-start(), calls=%async_computation.2 | async-start | bytes 5242880 | tf_op jit(solution)/shard_map/all_gather | solution.py:76
  69.4 19.7 %copy-start.15 = (s32[4]{0:T(128)S(1)}, s32[4]{0:T(128)}, u32[]{:S(2)}) copy-start(s32[4]{0:T(128)} %param.27) | copy-start | bytes 52
  69.4 21.2 %copy-start.14 = (bf16[512,2560]{1,0:T(8,128)(2,1)S(1)}, bf16[512,2560]{1,0:T(8,128)(2,1)}, u32[]{:S(2)}) copy-start(bf16[512,2560]{1,0:T(8,128)(2,1)} %param.22) | copy-start | bytes 7864324
  69.4 460.3 %all-to-all-start.1 = ((bf16[32,2,2,128,512]{4,3,2,1,0:T(8,128)(2,1)}), bf16[32,2,2,128,512]{4,3,2,1,0:T(8,128)(2,1)}, u32[]{:S(2)}, u32[]{:S(2)}) async-start(bf16[32,2,2,128,512]{4,3,2,1,0:T(8,128)(2,1)} %bitcast.315), calls=%async_computation.1 | async-start | bytes 33554432 | tf_op jit(solution)/shard_map/all_to_all | solution.py:83
  80.9 210.3 %collective-permute-start = (bf16[512,2,512]{0,2,1:T(8,128)(2,1)}, bf16[512,2,512]{0,2,1:T(8,128)(2,1)}, u32[]{:S(2)}, u32[]{:S(2)}) collective-permute-start(bf16[512,2,512]{0,2,1:T(8,128)(2,1)} %copy.142), channel_id=1, source_target_pairs={{0,1},{1,2},{2,3},{3,4},{4,5},{5,6},{6,7},{7,8},{8,9},{9,10},{10,1... | collective-permute-start | bytes 3145736 | tf_op jit(solution)/shard_map/ppermute | solution.py:13
  81.1 230.2 %collective-permute-start.1 = (bf16[512,2,512]{0,2,1:T(8,128)(2,1)}, bf16[512,2,512]{0,2,1:T(8,128)(2,1)}, u32[]{:S(2)}, u32[]{:S(2)}) collective-permute-start(bf16[512,2,512]{0,2,1:T(8,128)(2,1)} %copy.142), channel_id=1, source_target_pairs={{0,2},{1,3},{2,4},{3,5},{4,6},{5,7},{6,8},{7,9},{8,10},{9,11},{10,... | collective-permute-start | bytes 3145736 | tf_op jit(solution)/shard_map/ppermute | solution.py:13
  82.5 314.1 %collective-permute-start.2 = (bf16[512,2,512]{0,2,1:T(8,128)(2,1)}, bf16[512,2,512]{0,2,1:T(8,128)(2,1)}, u32[]{:S(2)}, u32[]{:S(2)}) collective-permute-start(bf16[512,2,512]{0,2,1:T(8,128)(2,1)} %copy.142), channel_id=1, source_target_pairs={{0,3},{1,4},{2,5},{3,6},{4,7},{5,8},{6,9},{7,10},{8,11},{9,12},{10... | collective-permute-start | bytes 3145736 | tf_op jit(solution)/shard_map/ppermute | solution.py:13
  84.5 338.8 %collective-permute-start.3 = (bf16[512,2,512]{0,2,1:T(8,128)(2,1)}, bf16[512,2,512]{0,2,1:T(8,128)(2,1)}, u32[]{:S(2)}, u32[]{:S(2)}) collective-permute-start(bf16[512,2,512]{0,2,1:T(8,128)(2,1)} %copy.142), channel_id=1, source_target_pairs={{0,4},{1,5},{2,6},{3,7},{4,8},{5,9},{6,10},{7,11},{8,12},{9,13},{1... | collective-permute-start | bytes 3145736 | tf_op jit(solution)/shard_map/ppermute | solution.py:13
  87.5 362.5 %collective-permute-start.4 = (bf16[512,2,512]{0,2,1:T(8,128)(2,1)}, bf16[512,2,512]{0,2,1:T(8,128)(2,1)}, u32[]{:S(2)}, u32[]{:S(2)}) collective-permute-start(bf16[512,2,512]{0,2,1:T(8,128)(2,1)} %copy.142), channel_id=1, source_target_pairs={{0,5},{1,6},{2,7},{3,8},{4,9},{5,10},{6,11},{7,12},{8,13},{9,14},{... | collective-permute-start | bytes 3145736 | tf_op jit(solution)/shard_map/ppermute | solution.py:13
  291.2 185.5 %collective-permute-start.5 = (bf16[512,2,512]{0,2,1:T(8,128)(2,1)}, bf16[512,2,512]{0,2,1:T(8,128)(2,1)}, u32[]{:S(2)}, u32[]{:S(2)}) collective-permute-start(bf16[512,2,512]{0,2,1:T(8,128)(2,1)} %copy.142), channel_id=1, source_target_pairs={{0,6},{1,7},{2,8},{3,9},{4,10},{5,11},{6,12},{7,13},{8,14},{9,15},... | collective-permute-start | bytes 3145736 | tf_op jit(solution)/shard_map/ppermute | solution.py:13
  311.3 192.3 %collective-permute-start.6 = (bf16[512,2,512]{0,2,1:T(8,128)(2,1)}, bf16[512,2,512]{0,2,1:T(8,128)(2,1)}, u32[]{:S(2)}, u32[]{:S(2)}) collective-permute-start(bf16[512,2,512]{0,2,1:T(8,128)(2,1)} %copy.142), channel_id=1, source_target_pairs={{0,7},{1,8},{2,9},{3,10},{4,11},{5,12},{6,13},{7,14},{8,15},{9,16}... | collective-permute-start | bytes 3145736 | tf_op jit(solution)/shard_map/ppermute | solution.py:13
  349.8 7.3 %copy-start.1 = (f32[4,512,4,128,5]{3,1,4,2,0:T(8,128)}, f32[4,512,4,128,5]{3,1,4,2,0:T(8,128)S(1)}, u32[]{:S(2)}) copy-start(f32[4,512,4,128,5]{3,1,4,2,0:T(8,128)S(1)} %get-tuple-element.465) | copy-start | bytes 62914564 | tf_op jit(solution)/shard_map/cond
  349.8 7.3 %copy-start.8 = (bf16[512,2,4,128]{3,0,2,1:T(8,128)(2,1)S(1)}, bf16[512,2,4,128]{3,0,2,1:T(8,128)(2,1)}, u32[]{:S(2)}) copy-start(bf16[512,2,4,128]{3,0,2,1:T(8,128)(2,1)} %copy.149) | copy-start | bytes 3145732 | tf_op jit(solution)/shard_map/cond
  376.4 7.3 %copy-start.2 = (f32[4,512,4,128,5]{3,1,4,2,0:T(8,128)}, f32[4,512,4,128,5]{3,1,4,2,0:T(8,128)S(1)}, u32[]{:S(2)}) copy-start(f32[4,512,4,128,5]{3,1,4,2,0:T(8,128)S(1)} %get-tuple-element.467) | copy-start | bytes 62914564 | tf_op jit(solution)/shard_map/cond
  376.4 7.3 %copy-start.9 = (bf16[512,2,4,128]{3,0,2,1:T(8,128)(2,1)S(1)}, bf16[512,2,4,128]{3,0,2,1:T(8,128)(2,1)}, u32[]{:S(2)}) copy-start(bf16[512,2,4,128]{3,0,2,1:T(8,128)(2,1)} %copy.152) | copy-start | bytes 3145732 | tf_op jit(solution)/shard_map/cond
  403.0 7.3 %copy-start.3 = (f32[4,512,4,128,5]{3,1,4,2,0:T(8,128)}, f32[4,512,4,128,5]{3,1,4,2,0:T(8,128)S(1)}, u32[]{:S(2)}) copy-start(f32[4,512,4,128,5]{3,1,4,2,0:T(8,128)S(1)} %get-tuple-element.469) | copy-start | bytes 62914564 | tf_op jit(solution)/shard_map/cond
  403.1 7.3 %copy-start.10 = (bf16[512,2,4,128]{3,0,2,1:T(8,128)(2,1)S(1)}, bf16[512,2,4,128]{3,0,2,1:T(8,128)(2,1)}, u32[]{:S(2)}) copy-start(bf16[512,2,4,128]{3,0,2,1:T(8,128)(2,1)} %copy.155) | copy-start | bytes 3145732 | tf_op jit(solution)/shard_map/cond
  429.7 7.3 %copy-start.4 = (f32[4,512,4,128,5]{3,1,4,2,0:T(8,128)}, f32[4,512,4,128,5]{3,1,4,2,0:T(8,128)S(1)}, u32[]{:S(2)}) copy-start(f32[4,512,4,128,5]{3,1,4,2,0:T(8,128)S(1)} %get-tuple-element.471) | copy-start | bytes 62914564 | tf_op jit(solution)/shard_map/cond
  429.8 7.3 %copy-start.11 = (bf16[512,2,4,128]{3,0,2,1:T(8,128)(2,1)S(1)}, bf16[512,2,4,128]{3,0,2,1:T(8,128)(2,1)}, u32[]{:S(2)}) copy-start(bf16[512,2,4,128]{3,0,2,1:T(8,128)(2,1)} %copy.158) | copy-start | bytes 3145732 | tf_op jit(solution)/shard_map/cond
  456.5 7.3 %copy-start.5 = (f32[4,512,4,128,5]{3,1,4,2,0:T(8,128)}, f32[4,512,4,128,5]{3,1,4,2,0:T(8,128)S(1)}, u32[]{:S(2)}) copy-start(f32[4,512,4,128,5]{3,1,4,2,0:T(8,128)S(1)} %get-tuple-element.473) | copy-start | bytes 62914564 | tf_op jit(solution)/shard_map/cond
  456.5 7.3 %copy-start.12 = (bf16[512,2,4,128]{3,0,2,1:T(8,128)(2,1)S(1)}, bf16[512,2,4,128]{3,0,2,1:T(8,128)(2,1)}, u32[]{:S(2)}) copy-start(bf16[512,2,4,128]{3,0,2,1:T(8,128)(2,1)} %copy.161) | copy-start | bytes 3145732 | tf_op jit(solution)/shard_map/cond
  483.4 7.3 %copy-start.6 = (f32[4,512,4,128,5]{3,1,4,2,0:T(8,128)}, f32[4,512,4,128,5]{3,1,4,2,0:T(8,128)S(1)}, u32[]{:S(2)}) copy-start(f32[4,512,4,128,5]{3,1,4,2,0:T(8,128)S(1)} %get-tuple-element.475) | copy-start | bytes 62914564 | tf_op jit(solution)/shard_map/cond
  483.5 7.3 %copy-start.13 = (bf16[512,2,4,128]{3,0,2,1:T(8,128)(2,1)S(1)}, bf16[512,2,4,128]{3,0,2,1:T(8,128)(2,1)}, u32[]{:S(2)}) copy-start(bf16[512,2,4,128]{3,0,2,1:T(8,128)(2,1)} %copy.164) | copy-start | bytes 3145732 | tf_op jit(solution)/shard_map/cond
  503.6 26.1 %copy-start.16 = (s32[4]{0:T(128)S(1)}, s32[4]{0:T(128)}, u32[]{:S(2)}) copy-start(s32[4]{0:T(128)} %param.27) | copy-start | bytes 52
  508.0 7.0 %copy-start.7 = (f32[4,512,4,128,5]{3,1,4,2,0:T(8,128)}, f32[4,512,4,128,5]{3,1,4,2,0:T(8,128)S(1)}, u32[]{:S(2)}) copy-start(f32[4,512,4,128,5]{3,1,4,2,0:T(8,128)S(1)} %get-tuple-element.477) | copy-start | bytes 62914564 | tf_op jit(solution)/shard_map/cond
  543.1 4.0 copy-start
  572.6 4.0 copy-start
  602.1 4.0 copy-start
  631.6 4.0 copy-start
Sparse Core Ops, SparseCore 0:
  9.0 50.6 all-gather.1
where the time goes:
time: 679 us; the launch traced here: 669 us
  waiting for transfers between devices  205 us (30%)
  matrix products  186 us (27%)
  local copies, waits for them, and re-layouts  132 us (19%)
  starting transfers between devices  58.8 us (9%)
  other arithmetic  56.5 us (8%)
  between operations  14.5 us (2%)
  blocking collectives  13.5 us (2%)
    ppermute x7, waiting for transfers between devices, from_behind(): return lax.ppermute(value, axis, pairs)  169 us
    dot_general x11, matrix products, absorb(): jnp.einsum(value_form, block_weights.astype(jnp.bfloat16), value_rows, pr...  124 us
    ppermute x7, starting transfers between devices, from_behind(): return lax.ppermute(value, axis, pairs)  50.9 us
    dot_general x11, matrix products, absorb(): jnp.einsum(score_form, queries, key_rows, preferred_element_type=jnp.floa...  40.1 us
    reduce_sum x11, other arithmetic, absorb(): new_sum = old_sum * rescale + jnp.sum(block_weights, axis=-1)  37.1 us
    all_gather x1, waiting for transfers between devices, local(): column = lax.all_gather(kv_cache, 'branch', axis=0, tiled=True)  35.7 us
    gather x4, local copies, waits for them, and re-layouts, advance(): blocks = received[where_now]  25.8 us
    cond x32, local copies, waits for them, and re-layouts  25.8 us
  transfers between devices with their start and end apart: 9, of which 2 were waited for; matrix products, arithmetic and copies ran while one was open for 31% of the time, Pallas kernels for 0%

commit v1 on v0

v1 whole, which is shorter than its diff:
```python
import functools
import math

import jax
import jax.numpy as jnp
from jax import lax
from jax.experimental import pallas as pl
from jax.experimental.pallas import tpu as pltpu
from jax.sharding import PartitionSpec as P

HEAD = 128
REQ_TILES = 32
EXP_SCALE = math.log2(math.e) / math.sqrt(HEAD)
CAP = 2


def request_table(dest_index, live_mask, count_dest, capacity, payload):
    onehot = (
        (dest_index[:, None] == jnp.arange(count_dest, dtype=jnp.int32)[None, :])
        & live_mask[:, None]
    ).astype(jnp.int32)
    rank_within = jnp.sum(onehot * (jnp.cumsum(onehot, axis=0) - 1), axis=1)
    position = dest_index * capacity + rank_within
    target = jnp.where(live_mask, position, -1)
    slot_ids = jnp.arange(count_dest * capacity, dtype=jnp.int32)
    requests = jnp.max(
        jnp.where(target[:, None] == slot_ids[None, :], payload[:, None], -1), axis=0
    )
    return (requests.reshape(count_dest, capacity), position)


def weigh(queries, keys, values_one, old_max, old_acc, mask):
    scores = lax.dot_general(
        queries, keys, (((1,), (1,)), ((), ())), preferred_element_type=jnp.float32
    )
    if mask is not None:
        scores = jnp.where(mask, scores, -jnp.inf)
    top = jnp.max(scores, axis=1, keepdims=True)
    new_max = top if old_max is None else jnp.maximum(old_max, top)
    weights = jnp.exp2((scores - new_max) * EXP_SCALE).astype(jnp.bfloat16)
    acc = jnp.dot(weights, values_one, preferred_element_type=jnp.float32)
    if old_max is not None:
        acc = acc + old_acc * jnp.exp2((old_max - new_max) * EXP_SCALE)
    return new_max, acc


def stack_heads(q_tile, repeat):
    return jnp.concatenate([q_tile[:, r * HEAD : (r + 1) * HEAD] for r in range(repeat)], axis=0)


def span_kernel(repeat, tile_rows, place_ref, q_ref, own_ref, *rest):
    earlier, (state_ref, key_buf, value_buf) = rest[:-3], rest[-3:]
    tiles = q_ref.shape[0] // tile_rows
    ones = jnp.ones((own_ref.shape[1], HEAD), jnp.bfloat16)
    for slot, ref in enumerate((own_ref, *earlier)):
        key_buf[slot] = ref[0]
        value_buf[slot, :, :HEAD] = ref[1]
        value_buf[slot, :, HEAD:] = ones
    wide = repeat * tile_rows
    for t in range(tiles):
        queries = stack_heads(q_ref[t * tile_rows : (t + 1) * tile_rows, :], repeat)
        seen = (t + 1) * tile_rows
        row = lax.rem(lax.broadcasted_iota(jnp.int32, (wide, seen), 0), tile_rows) + t * tile_rows
        col = lax.broadcasted_iota(jnp.int32, (wide, seen), 1)
        top, acc = weigh(
            queries, key_buf[0, :seen], value_buf[0, :seen], None, None, col <= row
        )
        state_ref[0, t, :, : 2 * HEAD] = acc
        state_ref[0, t, :, 2 * HEAD :] = jnp.broadcast_to(top, (wide, HEAD))

    def take(step, carry):
        slot, t = step // tiles + 1, lax.rem(step, tiles)
        rows = pl.ds(pl.multiple_of(t * tile_rows, tile_rows), tile_rows)
        queries = stack_heads(q_ref[rows, :], repeat)
        top, acc = weigh(
            queries,
            key_buf[slot],
            value_buf[slot],
            state_ref[0, t, :, 2 * HEAD : 2 * HEAD + 1],
            state_ref[0, t, :, : 2 * HEAD],
            None,
        )
        state_ref[0, t, :, : 2 * HEAD] = acc
        state_ref[0, t, :, 2 * HEAD :] = jnp.broadcast_to(top, (wide, HEAD))
        return carry

    lax.fori_loop(0, place_ref[0] * tiles, take, 0)


def span_attention(place, queries, own, earlier, tile_num):
    rows, width = queries.shape
    kv_heads = own.shape[2] // HEAD
    group = width // kv_heads
    repeat = group // HEAD
    tile_rows = rows // tile_num
    wide = repeat * tile_rows
    kv_spec = pl.BlockSpec((2, rows, HEAD), lambda g, place: (0, 0, g))
    slots = 1 + len(earlier)
    return pl.pallas_call(
        functools.partial(span_kernel, repeat, tile_rows),
        out_shape=jax.ShapeDtypeStruct((kv_heads, tile_num, wide, 3 * HEAD), jnp.float32),
        grid_spec=pltpu.PrefetchScalarGridSpec(
            num_scalar_prefetch=1,
            grid=(kv_heads,),
            in_specs=[pl.BlockSpec((rows, group), lambda g, place: (0, g))] + [kv_spec] * slots,
            out_specs=pl.BlockSpec((1, tile_num, wide, 3 * HEAD), lambda g, place: (g, 0, 0, 0)),
            scratch_shapes=[
                pltpu.VMEM((slots, rows, HEAD), jnp.bfloat16),
                pltpu.VMEM((slots, rows, 2 * HEAD), jnp.bfloat16),
            ],
        ),
        compiler_params=pltpu.CompilerParams(vmem_limit_bytes=56 * 2**20),
        cost_estimate=pl.CostEstimate(
            flops=4 * rows * width * rows * (slots // 2 + 1),
            bytes_accessed=rows * width * 2 + slots * rows * 4 * kv_heads * HEAD + rows * width * 12,
            transcendentals=rows * width // HEAD * rows * (slots // 2 + 1),
        ),
    )(place, queries, own, *earlier)


def listed_kernel(repeat, tile_rows, per_step, count_ref, pos_ref, q_ref, state_ref, block_ref, *rest):
    out_ref = rest[-1]
    t = pl.program_id(0)
    wide = repeat * tile_rows
    block_len = block_ref.shape[2]
    queries = stack_heads(q_ref[...], repeat)
    ones = jnp.ones((per_step * block_len, HEAD), jnp.bfloat16)
    count = count_ref[t]

    def take(step, carry):
        top, acc = carry
        first = step * per_step
        slots = [pos_ref[t, first + i] for i in range(per_step)]
        keys = jnp.concatenate([block_ref[s, 0] for s in slots], axis=0)
        values = jnp.concatenate([block_ref[s, 1] for s in slots], axis=0)
        col = lax.broadcasted_iota(jnp.int32, (1, per_step * block_len), 1)
        mask = col < (count - first) * block_len
        return weigh(
            queries, keys, jnp.concatenate([values, ones], axis=1), top, acc, mask
        )

    top, acc = state_ref[0, 0, :, 2 * HEAD : 2 * HEAD + 1], state_ref[0, 0, :, : 2 * HEAD]
    steps = (count + per_step - 1) // per_step
    top, acc = lax.fori_loop(0, steps, take, (top, acc))
    result = (acc[:, :HEAD] / acc[:, HEAD:]).astype(jnp.bfloat16)
    for r in range(repeat):
        out_ref[:, r * HEAD : (r + 1) * HEAD] = result[r * tile_rows : (r + 1) * tile_rows, :]


def listed_attention(head, counts, position, queries, state, blocks, partial_out):
    rows, width = queries.shape
    kv_heads, tile_num, wide, _ = state.shape
    group = width // kv_heads
    repeat = group // HEAD
    tile_rows = rows // tile_num
    in_specs = [
        pl.BlockSpec((tile_rows, group), lambda t, c, p: (t, head)),
        pl.BlockSpec((1, 1, wide, 3 * HEAD), lambda t, c, p: (head, t, 0, 0)),
        pl.BlockSpec(blocks.shape, lambda t, c, p: (0, 0, 0, 0)),
    ]
    operands = [counts, position, queries, state, blocks]
    aliases = {}
    if partial_out is not None:
        in_specs.append(pl.BlockSpec(memory_space=pl.ANY))
        operands.append(partial_out)
        aliases = {5: 0}
    keys = position.shape[1] * blocks.shape[2]
    return pl.pallas_call(
        functools.partial(listed_kernel, repeat, tile_rows, 4),
        out_shape=jax.ShapeDtypeStruct((rows, width), jnp.bfloat16),
        grid_spec=pltpu.PrefetchScalarGridSpec(
            num_scalar_prefetch=2,
            grid=(tile_num,),
            in_specs=in_specs,
            out_specs=pl.BlockSpec((tile_rows, group), lambda t, c, p: (t, head)),
        ),
        input_output_aliases=aliases,
        compiler_params=pltpu.CompilerParams(vmem_limit_bytes=40 * 2**20),
        cost_estimate=pl.CostEstimate(
            flops=4 * rows * group * keys,
            bytes_accessed=rows * group * 16 + blocks.size * 2,
            transcendentals=rows * repeat * keys,
        ),
    )(*operands)


def local(summary_q, summary_kv, kv_cache, block_slot, tile_blocks, tile_count):
    shards = lax.axis_size("ctx")
    groups = lax.axis_size("branch")
    devices = shards * groups
    tile_num, list_len = tile_blocks.shape
    blk_dev = kv_cache.shape[0]
    kv_heads = kv_cache.shape[3] // HEAD
    req_devs = REQ_TILES // tile_num
    entries = tile_blocks.reshape(-1)
    live_mask = (jnp.arange(list_len, dtype=jnp.int32)[None, :] < tile_count[:, None]).reshape(-1)
    block_ids = jnp.arange(block_slot.shape[0], dtype=jnp.int32)
    stored_at = jnp.sum(
        jnp.where(entries[:, None] == block_ids[None, :], block_slot[None, :], 0), axis=1
    )
    owner_dev = stored_at // blk_dev
    requests, position = request_table(
        owner_dev % shards,
        live_mask,
        shards,
        CAP,
        owner_dev // shards * blk_dev + stored_at % blk_dev,
    )
    asked = lax.all_to_all(requests, "ctx", split_axis=0, concat_axis=0, tiled=True)
    asked = jnp.maximum(asked, 0).reshape(-1)
    position = jnp.where(live_mask, position, 0).reshape(tile_num, list_len)
    flat_index = lax.axis_index("branch") * shards + lax.axis_index("ctx")
    place = (flat_index - 1 + req_devs) % req_devs
    own = summary_kv.transpose(1, 0, 2)
    earlier = []
    for distance in range(1, req_devs):
        pairs = [
            (source, (source + distance) % devices)
            for source in range(devices)
            if (source + distance - 1) % req_devs >= distance
        ]
        earlier.append(lax.ppermute(own, ("branch", "ctx"), pairs))
    state = span_attention(place[None], summary_q, own, earlier, tile_num)
    out = None
    for head in range(kv_heads):
        part = kv_cache[..., head * HEAD : (head + 1) * HEAD]
        column = lax.all_gather(part, "branch", axis=0, tiled=True)
        payload = column[asked]
        received = lax.all_to_all(payload, "ctx", split_axis=0, concat_axis=0, tiled=True)
        out = listed_attention(head, tile_count, position, summary_q, state, received, out)
    return out


def solution(mesh):
    in_specs = (
        P(("branch", "ctx"), None),
        P(("branch", "ctx"), None, None),
        P(("branch", "ctx"), None, None, None),
        P(),
        P(("branch", "ctx"), None),
        P(("branch", "ctx")),
    )
    out_specs = P(("branch", "ctx"), None)
    return jax.shard_map(local, mesh=mesh, in_specs=in_specs, out_specs=out_specs, check_vma=False)
```

time: 679 us -> 622 us (0.916)
  the two profiles are of different devices: /device:TPU:8 before, /device:TPU:16 now
where the time goes in v1:
time: 622 us; the launch traced here: 620 us
  waiting for transfers between devices  281 us (45%)
  Pallas kernels  251 us (40%)
  starting transfers between devices  38.6 us (6%)
  local copies, waits for them, and re-layouts  21.7 us (3%)
  between operations  13.3 us (2%)
  blocking collectives  12.5 us (2%)
    pallas_call x1, Pallas kernels, span_attention(): pl.pallas_call(functools.partial(span_kernel, repeat, tile_rows), out_sha...  180 us
    ppermute x7, waiting for transfers between devices, local(): earlier.append(lax.ppermute(own, ('branch', 'ctx'), pairs))  128 us
    all_gather x4, waiting for transfers between devices, local(): column = lax.all_gather(part, 'branch', axis=0, tiled=True)  89.8 us
    pallas_call x4, Pallas kernels, listed_attention(): pl.pallas_call(functools.partial(listed_kernel, repeat, tile_rows, 4), ou...  71.4 us
    all_to_all x4, waiting for transfers between devices, local(): lax.all_to_all(payload, 'ctx', split_axis=0, concat_axis=0, tiled=True)  60.9 us
    all_to_all x4, starting transfers between devices, local(): lax.all_to_all(payload, 'ctx', split_axis=0, concat_axis=0, tiled=True)  29.3 us
    gather x4, local copies, waits for them, and re-layouts, local(): payload = column[asked]  17.1 us
    all_to_all x1, blocking collectives, local(): lax.all_to_all(requests, 'ctx', split_axis=0, concat_axis=0, tiled=True)  12.5 us
  transfers between devices with their start and end apart: 15, of which 12 were waited for; matrix products, arithmetic and copies ran while one was open for 3% of the time, Pallas kernels for 38%

profile of v1, /device:TPU:16, one launch (start us, length us, event | category | flops | bytes accessed | tf_op | source)
XLA Modules:
  0.0 620.4 jit_solution(6568840913698995469)
XLA Ops:
  6.5 2.2 fusion.9
  11.8 12.5 %all_to_all.29 = s32[32,1,2]{2,1,0:T(1,128)S(1)} all-to-all(s32[32,1,2]{2,1,0:T(1,128)S(1)} %bitcast.13), channel_id=1, replica_groups=mesh['branch'=4,'ctx'=32] {'ctx'}, dimensions={0} | all-to-all | bytes 512 | tf_op jit(solution)/shard_map/all_to_all | solution.py:209
  24.5 11.1 %all-gather.11.cloned.1.call-done = bf16[16,2,128,128]{3,2,1,0:T(8,128)(2,1)} async-done(((bf16[4,2,128,128]{3,2,1,0:T(8,128)(2,1)}), bf16[16,2,128,128]{3,2,1,0:T(8,128)(2,1)}) %all-gather.11.cloned.1.call-update) | async-done | bytes 1048592 | tf_op jit(solution)/shard_map/all_gather | solution.py:227
  35.5 4.3 gather_fusion.3
  39.8 7.4 %all-to-all-start.4 = ((bf16[64,2,128,128]{3,2,1,0:T(8,128)(2,1)}), bf16[64,2,128,128]{3,2,1,0:T(8,128)(2,1)}, u32[]{:S(2)}, u32[]{:S(2)}) async-start(bf16[64,2,128,128]{3,2,1,0:T(8,128)(2,1)} %gather_fusion.3), calls=%async_computation.4 | async-start | bytes 8388608 | tf_op jit(solution)/shard_map/all_to_all | solution.py:229
  48.0 26.3 %all-gather.9.cloned.1.call-done = bf16[16,2,128,128]{3,2,1,0:T(8,128)(2,1)} async-done(((bf16[4,2,128,128]{3,2,1,0:T(8,128)(2,1)}), bf16[16,2,128,128]{3,2,1,0:T(8,128)(2,1)}) %all-gather.9.cloned.1.call-update) | async-done | bytes 1048592 | tf_op jit(solution)/shard_map/all_gather | solution.py:227
  74.3 4.3 gather_fusion.2
  78.6 20.2 %all-to-all-done.4.block_ref = bf16[64,2,128,128]{3,2,1,0:T(8,128)(2,1)} async-done(((bf16[64,2,128,128]{3,2,1,0:T(8,128)(2,1)}), bf16[64,2,128,128]{3,2,1,0:T(8,128)(2,1)}, u32[]{:S(2)}, u32[]{:S(2)}) %all-to-all-start.4) | async-done | bytes 4194336 | tf_op jit(solution)/shard_map/all_to_all | solution.py:229
  98.8 7.2 %all-to-all-start.3 = ((bf16[64,2,128,128]{3,2,1,0:T(8,128)(2,1)}), bf16[64,2,128,128]{3,2,1,0:T(8,128)(2,1)}, u32[]{:S(2)}, u32[]{:S(2)}) async-start(bf16[64,2,128,128]{3,2,1,0:T(8,128)(2,1)} %gather_fusion.2), calls=%async_computation.3 | async-start | bytes 8388608 | tf_op jit(solution)/shard_map/all_to_all | solution.py:229
  106.8 26.3 %all-gather.7.cloned.1.call-done = bf16[16,2,128,128]{3,2,1,0:T(8,128)(2,1)} async-done(((bf16[4,2,128,128]{3,2,1,0:T(8,128)(2,1)}), bf16[16,2,128,128]{3,2,1,0:T(8,128)(2,1)}) %all-gather.7.cloned.1.call-update) | async-done | bytes 1048592 | tf_op jit(solution)/shard_map/all_gather | solution.py:227
  133.1 4.3 gather_fusion.1
  137.3 20.2 %all-to-all-done.3.block_ref = bf16[64,2,128,128]{3,2,1,0:T(8,128)(2,1)} async-done(((bf16[64,2,128,128]{3,2,1,0:T(8,128)(2,1)}), bf16[64,2,128,128]{3,2,1,0:T(8,128)(2,1)}, u32[]{:S(2)}, u32[]{:S(2)}) %all-to-all-start.3) | async-done | bytes 4194336 | tf_op jit(solution)/shard_map/all_to_all | solution.py:229
  157.6 7.3 %all-to-all-start.2 = ((bf16[64,2,128,128]{3,2,1,0:T(8,128)(2,1)}), bf16[64,2,128,128]{3,2,1,0:T(8,128)(2,1)}, u32[]{:S(2)}, u32[]{:S(2)}) async-start(bf16[64,2,128,128]{3,2,1,0:T(8,128)(2,1)} %gather_fusion.1), calls=%async_computation.2 | async-start | bytes 8388608 | tf_op jit(solution)/shard_map/all_to_all | solution.py:229
  165.5 26.1 %all-gather.5.cloned.1.call-done = bf16[16,2,128,128]{3,2,1,0:T(8,128)(2,1)} async-done(((bf16[4,2,128,128]{3,2,1,0:T(8,128)(2,1)}), bf16[16,2,128,128]{3,2,1,0:T(8,128)(2,1)}) %all-gather.5.cloned.1.call-update) | async-done | bytes 1048592 | tf_op jit(solution)/shard_map/all_gather | solution.py:227
  191.6 4.3 gather_fusion
  195.9 20.4 %all-to-all-done.2.block_ref = bf16[64,2,128,128]{3,2,1,0:T(8,128)(2,1)} async-done(((bf16[64,2,128,128]{3,2,1,0:T(8,128)(2,1)}), bf16[64,2,128,128]{3,2,1,0:T(8,128)(2,1)}, u32[]{:S(2)}, u32[]{:S(2)}) %all-to-all-start.2) | async-done | bytes 4194336 | tf_op jit(solution)/shard_map/all_to_all | solution.py:229
  216.4 7.3 %all-to-all-start.1 = ((bf16[64,2,128,128]{3,2,1,0:T(8,128)(2,1)}), bf16[64,2,128,128]{3,2,1,0:T(8,128)(2,1)}, u32[]{:S(2)}, u32[]{:S(2)}) async-start(bf16[64,2,128,128]{3,2,1,0:T(8,128)(2,1)} %gather_fusion), calls=%async_computation.1 | async-start | bytes 8388608 | tf_op jit(solution)/shard_map/all_to_all | solution.py:229
  223.9 1.3 collective-permute-start
  225.2 1.3 collective-permute-start.1
  226.5 1.3 collective-permute-start.2
  227.8 1.3 collective-permute-start.3
  229.1 1.3 collective-permute-start.4
  230.4 64.4 %collective-permute-done.rest_0_ = bf16[2,512,512]{2,1,0:T(8,128)(2,1)S(1)} collective-permute-done((bf16[2,512,512]{2,1,0:T(8,128)(2,1)S(1)}, bf16[2,512,512]{2,1,0:T(8,128)(2,1)S(1)}, u32[]{:S(2)}, u32[]{:S(2)}) %collective-permute-start) | collective-permute-done | bytes 1048608 | tf_op jit(solution)/shard_map/ppermute | solution.py:222
  294.8 1.3 collective-permute-start.5
  297.1 1.5 collective-permute-start.6
  298.8 56.8 %collective-permute-done.2.rest_2_ = bf16[2,512,512]{2,1,0:T(8,128)(2,1)S(1)} collective-permute-done((bf16[2,512,512]{2,1,0:T(8,128)(2,1)S(1)}, bf16[2,512,512]{2,1,0:T(8,128)(2,1)S(1)}, u32[]{:S(2)}, u32[]{:S(2)}) %collective-permute-start.2) | collective-permute-done | bytes 1048608 | tf_op jit(solution)/shard_map/ppermute | solution.py:222
  356.6 5.2 collective-permute-done.4.rest_4_
  362.4 180.1 %shard_map.64.state_ref = f32[4,4,640,384]{3,2,1,0:T(8,128)} custom-call(s32[1]{0:T(128)} %bitcast.place_ref, bf16[512,2560]{1,0:T(8,128)(2,1)} %q_ref.9, bf16[2,512,512]{2,1,0:T(8,128)(2,1)} %bitcast.12, bf16[2,512,512]{2,1,0:T(8,128)(2,1)} %copy-done.4, bf16[2,512,512]{2,1,0:T(8,128)(2,1)} %copy-done.5, bf16[2,512,512]{2,1,0:T(8,128)(2,1)} %copy-done.6, ...), custom_call_target="tpu_custom_call" | custom-call | flops 13421772800 | bytes 26738688 | tf_op jit(solution)/shard_map/pallas_call | solution.py:99
  542.5 17.8 %shard_map.65.rest_0_ = bf16[512,2560]{1,0:T(8,128)(2,1)} custom-call(s32[4]{0:T(128)S(1)} %copy-done.1, s32[4,8]{1,0:T(4,128)S(1)} %fusion.6.pos_ref, bf16[512,2560]{1,0:T(8,128)(2,1)S(1)} %copy-done, f32[4,4,640,384]{3,2,1,0:T(8,128)} %shard_map.64.state_ref, bf16[64,2,128,128]{3,2,1,0:T(8,128)(2,1)} %all-to-all-done.4.block_ref), custom_call_target="tpu_custom_call" | custom-call | flops 1342177280 | bytes 9437184 | tf_op jit(solution)/shard_map/pallas_call | solution.py:168
  560.3 17.8 %shard_map.66.rest_0_ = bf16[512,2560]{1,0:T(8,128)(2,1)} custom-call(s32[4]{0:T(128)S(1)} %copy-done.1, s32[4,8]{1,0:T(4,128)S(1)} %fusion.6.pos_ref, bf16[512,2560]{1,0:T(8,128)(2,1)S(1)} %copy-done, f32[4,4,640,384]{3,2,1,0:T(8,128)} %shard_map.64.state_ref, bf16[64,2,128,128]{3,2,1,0:T(8,128)(2,1)} %all-to-all-done.3.block_ref, ...), custom_call_target="tpu_custom_call", output_to_operand_aliasing={{}: (5, {})} | custom-call | flops 1342177280 | bytes 9437184 | tf_op jit(solution)/shard_map/pallas_call | solution.py:168
  578.2 17.8 %shard_map.67.rest_0_ = bf16[512,2560]{1,0:T(8,128)(2,1)} custom-call(s32[4]{0:T(128)S(1)} %copy-done.1, s32[4,8]{1,0:T(4,128)S(1)} %fusion.6.pos_ref, bf16[512,2560]{1,0:T(8,128)(2,1)S(1)} %copy-done, f32[4,4,640,384]{3,2,1,0:T(8,128)} %shard_map.64.state_ref, bf16[64,2,128,128]{3,2,1,0:T(8,128)(2,1)} %all-to-all-done.2.block_ref, ...), custom_call_target="tpu_custom_call", output_to_operand_aliasing={{}: (5, {})} | custom-call | flops 1342177280 | bytes 9437184 | tf_op jit(solution)/shard_map/pallas_call | solution.py:168
  596.0 17.8 %shard_map.68 = bf16[512,2560]{1,0:T(8,128)(2,1)} custom-call(s32[4]{0:T(128)S(1)} %copy-done.1, s32[4,8]{1,0:T(4,128)S(1)} %fusion.6.pos_ref, bf16[512,2560]{1,0:T(8,128)(2,1)S(1)} %copy-done, f32[4,4,640,384]{3,2,1,0:T(8,128)} %shard_map.64.state_ref, bf16[64,2,128,128]{3,2,1,0:T(8,128)(2,1)} %all-to-all-done.1.block_ref, ...), custom_call_target="tpu_custom_call", output_to_operand_aliasing={{}: (5, {})} | custom-call | flops 1342177280 | bytes 9437184 | tf_op jit(solution)/shard_map/pallas_call | solution.py:168
  (46 shorter events, 8.2 us)
Async XLA Ops:
  6.5 29.0 %all-gather.11.cloned.1.call-start = ((), (), s32[]{:S(2)}) async-start(), calls=%async_computation.8 | async-start | bytes 1310720 | tf_op jit(solution)/shard_map/all_gather | solution.py:227
  39.8 59.0 %all-to-all-start.4 = ((bf16[64,2,128,128]{3,2,1,0:T(8,128)(2,1)}), bf16[64,2,128,128]{3,2,1,0:T(8,128)(2,1)}, u32[]{:S(2)}, u32[]{:S(2)}) async-start(bf16[64,2,128,128]{3,2,1,0:T(8,128)(2,1)} %gather_fusion.3), calls=%async_computation.4 | async-start | bytes 8388608 | tf_op jit(solution)/shard_map/all_to_all | solution.py:229
  47.2 27.0 %all-gather.9.cloned.1.call-start = ((), (), s32[]{:S(2)}) async-start(), calls=%async_computation.7 | async-start | bytes 1310720 | tf_op jit(solution)/shard_map/all_gather | solution.py:227
  98.8 58.7 %all-to-all-start.3 = ((bf16[64,2,128,128]{3,2,1,0:T(8,128)(2,1)}), bf16[64,2,128,128]{3,2,1,0:T(8,128)(2,1)}, u32[]{:S(2)}, u32[]{:S(2)}) async-start(bf16[64,2,128,128]{3,2,1,0:T(8,128)(2,1)} %gather_fusion.2), calls=%async_computation.3 | async-start | bytes 8388608 | tf_op jit(solution)/shard_map/all_to_all | solution.py:229
  106.1 27.0 %all-gather.7.cloned.1.call-start = ((), (), s32[]{:S(2)}) async-start(), calls=%async_computation.6 | async-start | bytes 1310720 | tf_op jit(solution)/shard_map/all_gather | solution.py:227
  157.6 58.8 %all-to-all-start.2 = ((bf16[64,2,128,128]{3,2,1,0:T(8,128)(2,1)}), bf16[64,2,128,128]{3,2,1,0:T(8,128)(2,1)}, u32[]{:S(2)}, u32[]{:S(2)}) async-start(bf16[64,2,128,128]{3,2,1,0:T(8,128)(2,1)} %gather_fusion.1), calls=%async_computation.2 | async-start | bytes 8388608 | tf_op jit(solution)/shard_map/all_to_all | solution.py:229
  164.9 26.7 %all-gather.5.cloned.1.call-start = ((), (), s32[]{:S(2)}) async-start(), calls=%async_computation.5 | async-start | bytes 1310720 | tf_op jit(solution)/shard_map/all_gather | solution.py:227
  195.9 27.8 %copy-start.2 = (bf16[512,2,512]{2,1,0:T(2,128)(2,1)S(1)}, bf16[512,2,512]{2,1,0:T(2,128)(2,1)}, u32[]{:S(2)}) copy-start(bf16[512,2,512]{2,1,0:T(2,128)(2,1)} %param.7) | copy-start | bytes 3145732
  195.9 102.8 %copy-start.1 = (s32[4]{0:T(128)S(1)}, s32[4]{0:T(128)}, u32[]{:S(2)}) copy-start(s32[4]{0:T(128)} %count_ref.7) | copy-start | bytes 52
  216.4 379.7 %all-to-all-start.1 = ((bf16[64,2,128,128]{3,2,1,0:T(8,128)(2,1)}), bf16[64,2,128,128]{3,2,1,0:T(8,128)(2,1)}, u32[]{:S(2)}, u32[]{:S(2)}) async-start(bf16[64,2,128,128]{3,2,1,0:T(8,128)(2,1)} %gather_fusion), calls=%async_computation.1 | async-start | bytes 8388608 | tf_op jit(solution)/shard_map/all_to_all | solution.py:229
  223.9 138.5 %copy-start.3 = (bf16[512,2,512]{2,0,1:T(8,128)(2,1)}, bf16[512,2,512]{2,0,1:T(8,128)(2,1)S(1)}, u32[]{:S(2)}) copy-start(bf16[512,2,512]{2,0,1:T(8,128)(2,1)S(1)} %copy.17) | copy-start | bytes 3145732
  223.9 70.9 %collective-permute-start = (bf16[2,512,512]{2,1,0:T(8,128)(2,1)S(1)}, bf16[2,512,512]{2,1,0:T(8,128)(2,1)S(1)}, u32[]{:S(2)}, u32[]{:S(2)}) collective-permute-start(bf16[2,512,512]{2,1,0:T(8,128)(2,1)S(1)} %bitcast.5), channel_id=1, source_target_pairs={{1,2},{2,3},{3,4},{4,5},{5,6},{6,7},{7,8},{9,10},{10,11},{11,12},{... | collective-permute-start | bytes 3145736 | tf_op jit(solution)/shard_map/ppermute | solution.py:222
  225.2 70.9 %collective-permute-start.1 = (bf16[2,512,512]{2,1,0:T(8,128)(2,1)S(1)}, bf16[2,512,512]{2,1,0:T(8,128)(2,1)S(1)}, u32[]{:S(2)}, u32[]{:S(2)}) collective-permute-start(bf16[2,512,512]{2,1,0:T(8,128)(2,1)S(1)} %bitcast.6), channel_id=1, source_target_pairs={{1,3},{2,4},{3,5},{4,6},{5,7},{6,8},{9,11},{10,12},{11,13},{12,14}... | collective-permute-start | bytes 3145736 | tf_op jit(solution)/shard_map/ppermute | solution.py:222
  226.5 129.1 %collective-permute-start.2 = (bf16[2,512,512]{2,1,0:T(8,128)(2,1)S(1)}, bf16[2,512,512]{2,1,0:T(8,128)(2,1)S(1)}, u32[]{:S(2)}, u32[]{:S(2)}) collective-permute-start(bf16[2,512,512]{2,1,0:T(8,128)(2,1)S(1)} %bitcast.7), channel_id=1, source_target_pairs={{1,4},{2,5},{3,6},{4,7},{5,8},{9,12},{10,13},{11,14},{12,15},{13,1... | collective-permute-start | bytes 3145736 | tf_op jit(solution)/shard_map/ppermute | solution.py:222
  227.8 128.8 %collective-permute-start.3 = (bf16[2,512,512]{2,1,0:T(8,128)(2,1)S(1)}, bf16[2,512,512]{2,1,0:T(8,128)(2,1)}, u32[]{:S(2)}, u32[]{:S(2)}) collective-permute-start(bf16[2,512,512]{2,1,0:T(8,128)(2,1)S(1)} %bitcast.8), channel_id=1, source_target_pairs={{1,5},{2,6},{3,7},{4,8},{9,13},{10,14},{11,15},{12,16},{17,21},{18... | collective-permute-start | bytes 3145736 | tf_op jit(solution)/shard_map/ppermute | solution.py:222
  229.1 132.7 %collective-permute-start.4 = (bf16[2,512,512]{2,1,0:T(8,128)(2,1)S(1)}, bf16[2,512,512]{2,1,0:T(8,128)(2,1)}, u32[]{:S(2)}, u32[]{:S(2)}) collective-permute-start(bf16[2,512,512]{2,1,0:T(8,128)(2,1)S(1)} %bitcast.9), channel_id=1, source_target_pairs={{1,6},{2,7},{3,8},{9,14},{10,15},{11,16},{17,22},{18,23},{19,24},{... | collective-permute-start | bytes 3145736 | tf_op jit(solution)/shard_map/ppermute | solution.py:222
  294.8 3.8 copy-start.4
  294.8 67.6 %collective-permute-start.5 = (bf16[2,512,512]{2,1,0:T(8,128)(2,1)S(1)}, bf16[2,512,512]{2,1,0:T(8,128)(2,1)}, u32[]{:S(2)}, u32[]{:S(2)}) collective-permute-start(bf16[2,512,512]{2,1,0:T(8,128)(2,1)S(1)} %bitcast.10), channel_id=1, source_target_pairs={{1,7},{2,8},{9,15},{10,16},{17,23},{18,24},{25,31},{26,32},{33,39}... | collective-permute-start | bytes 3145736 | tf_op jit(solution)/shard_map/ppermute | solution.py:222
  296.1 1.0 copy-start.5
  297.1 65.3 %collective-permute-start.6 = (bf16[2,512,512]{2,1,0:T(8,128)(2,1)S(1)}, bf16[2,512,512]{2,1,0:T(8,128)(2,1)}, u32[]{:S(2)}, u32[]{:S(2)}) collective-permute-start(bf16[2,512,512]{2,1,0:T(8,128)(2,1)S(1)} %bitcast.11), channel_id=1, source_target_pairs={{1,8},{9,16},{17,24},{25,32},{33,40},{41,48},{49,56},{57,64},{65,7... | collective-permute-start | bytes 3145736 | tf_op jit(solution)/shard_map/ppermute | solution.py:222
  355.6 6.8 %copy-start.6 = (bf16[2,512,512]{2,1,0:T(8,128)(2,1)}, bf16[2,512,512]{2,1,0:T(8,128)(2,1)S(1)}, u32[]{:S(2)}) copy-start(bf16[2,512,512]{2,1,0:T(8,128)(2,1)S(1)} %collective-permute-done.2.rest_2_) | copy-start | bytes 3145732
  362.4 180.1 %copy-start = (bf16[512,2560]{1,0:T(8,128)(2,1)S(1)}, bf16[512,2560]{1,0:T(8,128)(2,1)}, u32[]{:S(2)}) copy-start(bf16[512,2560]{1,0:T(8,128)(2,1)} %q_ref.9) | copy-start | bytes 7864324
Sparse Core Ops, SparseCore 0:
  9.0 26.5 all-gather.10
  49.7 24.5 all-gather.8
  108.5 24.5 all-gather.6
  167.0 24.5 all-gather.4

commit v2 on v1

v2 whole, which is shorter than its diff:
```python
import functools
import math

import jax
import jax.numpy as jnp
from jax import lax
from jax.experimental import pallas as pl
from jax.experimental.pallas import tpu as pltpu
from jax.sharding import Mesh
from jax.sharding import PartitionSpec as P


HEAD = 128
REQ_TILES = 32
EXP_SCALE = math.log2(math.e) / math.sqrt(HEAD)
ALL = ("z", "y", "x", "c")
PLANE = ("y", "x", "c")
CAP = 2
CHUNKS = ((0,), (1, 2), (3,))
PLAN = ((), ((0, 1), (2, 3), 0), (1, 2, 3))


def request_table(dest_index, live_mask, count_dest, capacity, payload):
    onehot = (
        (dest_index[:, None] == jnp.arange(count_dest, dtype=jnp.int32)[None, :])
        & live_mask[:, None]
    ).astype(jnp.int32)
    rank_within = jnp.sum(onehot * (jnp.cumsum(onehot, axis=0) - 1), axis=1)
    target = jnp.where(live_mask, dest_index * capacity + rank_within, -1)
    slot_ids = jnp.arange(count_dest * capacity, dtype=jnp.int32)
    requests = jnp.max(
        jnp.where(target[:, None] == slot_ids[None, :], payload[:, None], 0), axis=0
    )
    return (requests.reshape(count_dest, capacity), dest_index * capacity + rank_within)


def score(queries, keys):
    return lax.dot_general(
        queries, keys, (((1,), (1,)), ((), ())), preferred_element_type=jnp.float32
    )


def weigh(scores, values_one, old_max, old_acc, masks):
    pieces = [scores[:, i : i + HEAD] for i in range(0, scores.shape[1], HEAD)]
    pieces = [
        piece if mask is None else jnp.where(mask, piece, -jnp.inf)
        for piece, mask in zip(pieces, masks, strict=True)
    ]
    top = jnp.max(functools.reduce(jnp.maximum, pieces), axis=1, keepdims=True)
    top = jnp.broadcast_to(top, pieces[0].shape)
    new_max = top if old_max is None else jnp.maximum(old_max, top)
    weights = [
        jnp.exp2((piece - new_max) * EXP_SCALE).astype(jnp.bfloat16) for piece in pieces
    ]
    acc = jnp.dot(
        jnp.concatenate(weights, axis=1), values_one, preferred_element_type=jnp.float32
    )
    if old_max is None:
        return new_max, acc[:, :HEAD], acc[:, HEAD:]
    fade = jnp.exp2((old_max - new_max) * EXP_SCALE)
    total, row_sum = old_acc
    return new_max, acc[:, :HEAD] + total * fade, acc[:, HEAD:] + row_sum * fade


def stack_heads(q_tile, repeat):
    return jnp.concatenate([q_tile[:, r * HEAD : (r + 1) * HEAD] for r in range(repeat)], axis=0)


def span_kernel(repeat, tile_rows, place_ref, q_ref, own_ref, *rest):
    earlier, (state_ref, key_buf, value_buf) = rest[:-3], rest[-3:]
    tiles = q_ref.shape[0] // tile_rows
    ones = jnp.ones((own_ref.shape[1], HEAD), jnp.bfloat16)
    other_ref, same_refs, first_ref = earlier[0], earlier[1:-1], earlier[-1]
    spans = [own_ref]
    for i, same_ref in enumerate(same_refs):
        spans += [other_ref.at[i], same_ref]
    for slot, ref in enumerate((*spans, first_ref)):
        key_buf[slot] = ref[0]
        value_buf[slot, :, :HEAD] = ref[1]
        value_buf[slot, :, HEAD:] = ones
    wide = repeat * tile_rows

    def own_scores(t):
        queries = stack_heads(q_ref[t * tile_rows : (t + 1) * tile_rows, :], repeat)
        return score(queries, key_buf[0, : (t + 1) * tile_rows])

    def put(t, state):
        for i, part in enumerate((*state[1:], state[0])):
            state_ref[0, t, :, i * HEAD : (i + 1) * HEAD] = part

    row = lax.rem(lax.broadcasted_iota(jnp.int32, (wide, tile_rows), 0), tile_rows)
    diagonal = lax.broadcasted_iota(jnp.int32, (wide, tile_rows), 1) <= row
    ahead = own_scores(0)
    for t in range(tiles):
        scores = ahead
        if t + 1 < tiles:
            ahead = own_scores(t + 1)
        masks = [None] * t + [diagonal]
        put(t, weigh(scores, value_buf[0, : (t + 1) * tile_rows], None, None, masks))

    def take(slot, carry):
        keys, values_one = key_buf[slot], value_buf[slot]

        def slot_scores(t):
            queries = stack_heads(q_ref[t * tile_rows : (t + 1) * tile_rows, :], repeat)
            return score(queries, keys)

        ahead = slot_scores(0)
        for t in range(tiles):
            scores = ahead
            if t + 1 < tiles:
                ahead = slot_scores(t + 1)
            old = [state_ref[0, t, :, i * HEAD : (i + 1) * HEAD] for i in range(3)]
            put(t, weigh(scores, values_one, old[2], old[:2], [None] * tiles))
        return carry

    lax.fori_loop(1, place_ref[0] + 1, take, 0)


def span_attention(heads, place, queries, own, earlier, tile_num):
    rows, width = queries.shape
    kv_heads = own.shape[2] // HEAD
    group = width // kv_heads
    repeat = group // HEAD
    tile_rows = rows // tile_num
    wide = repeat * tile_rows
    kv_spec = pl.BlockSpec((2, rows, HEAD), lambda g, place: (0, 0, heads[0] + g))
    other_spec = pl.BlockSpec(
        (earlier[0].shape[0], 2, rows, HEAD), lambda g, place: (0, 0, 0, heads[0] + g)
    )
    slots = len(earlier) + earlier[0].shape[0]
    return pl.pallas_call(
        functools.partial(span_kernel, repeat, tile_rows),
        out_shape=jax.ShapeDtypeStruct((len(heads), tile_num, wide, 3 * HEAD), jnp.float32),
        grid_spec=pltpu.PrefetchScalarGridSpec(
            num_scalar_prefetch=1,
            grid=(len(heads),),
            in_specs=[pl.BlockSpec((rows, group), lambda g, place: (0, heads[0] + g))]
            + [kv_spec, other_spec] + [kv_spec] * (len(earlier) - 1),
            out_specs=pl.BlockSpec((1, tile_num, wide, 3 * HEAD), lambda g, place: (g, 0, 0, 0)),
            scratch_shapes=[
                pltpu.VMEM((slots, rows, HEAD), jnp.bfloat16),
                pltpu.VMEM((slots, rows, 2 * HEAD), jnp.bfloat16),
            ],
        ),
        compiler_params=pltpu.CompilerParams(vmem_limit_bytes=56 * 2**20),
        cost_estimate=pl.CostEstimate(
            flops=4 * len(heads) * rows * group * rows * slots,
            bytes_accessed=len(heads) * (rows * group * 14 + slots * rows * 4 * HEAD),
            transcendentals=len(heads) * rows * repeat * rows * slots,
        ),
    )(place, queries, own, *earlier)


def listed_kernel(repeat, tile_rows, count_ref, pos_ref, q_ref, state_ref, block_ref, *rest):
    out_ref = rest[-1]
    tiles = q_ref.shape[0] // tile_rows
    list_len = pos_ref.shape[1]
    block_len = block_ref.shape[2]
    ones = jnp.ones((list_len * block_len, HEAD), jnp.bfloat16)

    def listed(t, kind):
        return jnp.concatenate([block_ref[pos_ref[t, i], kind] for i in range(list_len)], axis=0)

    def tile_scores(t):
        queries = stack_heads(q_ref[t * tile_rows : (t + 1) * tile_rows, :], repeat)
        return score(queries, listed(t, 0))

    ahead = tile_scores(0)
    for t in range(tiles):
        scores = ahead
        if t + 1 < tiles:
            ahead = tile_scores(t + 1)
        masks = [i < count_ref[t] for i in range(list_len)]
        old = [state_ref[0, t, :, i * HEAD : (i + 1) * HEAD] for i in range(3)]
        values_one = jnp.concatenate([listed(t, 1), ones], axis=1)
        _, total, row_sum = weigh(scores, values_one, old[2], old[:2], masks)
        result = (total / row_sum).astype(jnp.bfloat16)
        for r in range(repeat):
            out_ref[t * tile_rows : (t + 1) * tile_rows, r * HEAD : (r + 1) * HEAD] = result[
                r * tile_rows : (r + 1) * tile_rows, :
            ]


def listed_attention(head, state_row, counts, position, queries, state, blocks, lane, partial_out):
    rows, width = queries.shape
    _, tile_num, wide, _ = state.shape
    group = wide * tile_num // rows * HEAD
    repeat = group // HEAD
    tile_rows = rows // tile_num
    in_specs = [
        pl.BlockSpec((rows, group), lambda t, c, p: (0, head)),
        pl.BlockSpec((1, tile_num, wide, 3 * HEAD), lambda t, c, p: (state_row, 0, 0, 0)),
        pl.BlockSpec((*blocks.shape[:3], HEAD), lambda t, c, p: (0, 0, 0, lane)),
    ]
    operands = [counts, position, queries, state, blocks]
    aliases = {}
    if partial_out is not None:
        in_specs.append(pl.BlockSpec(memory_space=pl.ANY))
        operands.append(partial_out)
        aliases = {5: 0}
    keys = position.shape[1] * blocks.shape[2]
    return pl.pallas_call(
        functools.partial(listed_kernel, repeat, tile_rows),
        out_shape=jax.ShapeDtypeStruct((rows, width), jnp.bfloat16),
        grid_spec=pltpu.PrefetchScalarGridSpec(
            num_scalar_prefetch=2,
            grid=(1,),
            in_specs=in_specs,
            out_specs=pl.BlockSpec((rows, group), lambda t, c, p: (0, head)),
        ),
        input_output_aliases=aliases,
        compiler_params=pltpu.CompilerParams(vmem_limit_bytes=40 * 2**20),
        cost_estimate=pl.CostEstimate(
            flops=4 * rows * group * keys,
            bytes_accessed=rows * group * 16 + blocks.size * 2,
            transcendentals=rows * repeat * keys,
        ),
    )(*operands)


def local(summary_q, summary_kv, kv_cache, block_slot, tile_blocks, tile_count):
    plane, devices = lax.axis_size(PLANE), lax.axis_size(ALL)
    tile_num, list_len = tile_blocks.shape
    blk_dev = kv_cache.shape[0]
    req_devs = REQ_TILES // tile_num
    flat_index = lax.axis_index(ALL)
    entries = tile_blocks.reshape(-1)
    live_mask = (jnp.arange(list_len, dtype=jnp.int32)[None, :] < tile_count[:, None]).reshape(-1)
    block_ids = jnp.arange(block_slot.shape[0], dtype=jnp.int32)
    stored_at = jnp.sum(
        jnp.where(entries[:, None] == block_ids[None, :], block_slot[None, :], 0), axis=1
    )
    owner_dev = stored_at // blk_dev
    requests, position = request_table(
        owner_dev % plane,
        live_mask,
        plane,
        CAP,
        owner_dev // plane * blk_dev + stored_at % blk_dev,
    )
    asked = lax.all_to_all(requests, PLANE, split_axis=0, concat_axis=0, tiled=True)
    position = jnp.where(live_mask, position, 0).reshape(tile_num, list_len)
    place = (flat_index - 1 + req_devs) % req_devs
    own, asked = lax.optimization_barrier((summary_kv.transpose(1, 0, 2), asked))
    asked = asked.reshape(-1)

    def ahead(value, distance, takes):
        pairs = [
            (source, (source + distance) % devices)
            for source in range(devices)
            if takes((source - 1) % req_devs)
        ]
        return lax.ppermute(value, ALL, pairs)

    core = lax.axis_index("c")
    second = ahead(own, 2, lambda p: p + 2 <= req_devs)
    sixth = ahead(own, 6, lambda p: p + 6 <= req_devs)
    first = ahead(own, req_devs - 1, lambda p: p == 0)
    fourth = ahead(second, 2, lambda p: 2 <= p <= req_devs - 2)
    same = [second, fourth, sixth]
    give = [jnp.where(core == 0, a, b) for a, b in zip([own, *same[:-1]], same, strict=True)]
    other = lax.ppermute(jnp.stack(give), "c", [(0, 1), (1, 0)])
    earlier = [other, *same, first]
    columns = [
        lax.all_gather(
            kv_cache[..., heads[0] * HEAD : (heads[-1] + 1) * HEAD], "z", axis=0, tiled=True
        )
        for heads in CHUNKS
    ]
    states, received, out = [], {}, None
    for turn, heads in enumerate(CHUNKS):
        column = columns[turn]
        if turn > 0:
            column, states, out = lax.optimization_barrier((column, states, out))
        arrived = lax.all_to_all(column[asked], PLANE, split_axis=0, concat_axis=0, tiled=True)
        for i, head in enumerate(heads):
            received[head] = (arrived, i)
        for task in PLAN[turn]:
            if isinstance(task, tuple):
                state = span_attention(task, place[None], summary_q, own, earlier, tile_num)
                states = states + [state]
            else:
                out = listed_attention(
                    task,
                    task % 2,
                    tile_count,
                    position,
                    summary_q,
                    states[task // 2],
                    *received[task],
                    out,
                )
    return out


def solution(mesh):
    grid = Mesh(mesh.devices.reshape(4, 4, 4, 2), ALL)
    in_specs = (P(ALL, None), P(ALL, None, None), P(ALL, None, None, None), P(), P(ALL, None), P(ALL))

    return jax.shard_map(local, mesh=grid, in_specs=in_specs, out_specs=P(ALL, None), check_vma=False)
```

time: 622 us -> 449 us (0.72)
  the two profiles are of different devices: /device:TPU:16 before, /device:TPU:8 now
where the time goes in v2:
time: 449 us; the launch traced here: 445 us
  waiting for transfers between devices  262 us (58%)
  Pallas kernels  96.3 us (21%)
  starting transfers between devices  38.5 us (9%)
  local copies, waits for them, and re-layouts  29.1 us (6%)
  between operations  13.3 us (3%)
  other arithmetic  5.64 us (1%)
    ppermute x4, waiting for transfers between devices, ahead(): return lax.ppermute(value, ALL, pairs)  175 us
    pallas_call x2, Pallas kernels, span_attention(): pl.pallas_call(functools.partial(span_kernel, repeat, tile_rows), out_sha...  65.5 us
    all_gather x3, waiting for transfers between devices, local(): lax.all_gather(kv_cache[..., heads[0] * HEAD:(heads[-1] + 1) * HEAD], 'z'...  42.3 us
    all_to_all x3, waiting for transfers between devices, local(): lax.all_to_all(column[asked], PLANE, split_axis=0, concat_axis=0, tiled=T...  40.6 us
    pallas_call x4, Pallas kernels, listed_attention(): pl.pallas_call(functools.partial(listed_kernel, repeat, tile_rows), out_s...  30.8 us
    all_to_all x3, starting transfers between devices, local(): lax.all_to_all(column[asked], PLANE, split_axis=0, concat_axis=0, tiled=T...  25.5 us
    gather x3, local copies, waits for them, and re-layouts, local(): column[asked]  15.5 us
  transfers between devices with their start and end apart: 12, of which 9 were waited for; matrix products, arithmetic and copies ran while one was open for 5% of the time, Pallas kernels for 20%

profile of v2, /device:TPU:8, one launch (start us, length us, event | category | flops | bytes accessed | tf_op | source)
XLA Modules:
  0.0 445.1 jit_solution(7224417816784810780)
XLA Ops:
  6.5 1.9 fusion.10
  12.1 7.5 %all-to-all-start = ((s32[32,1,2]{2,1,0:T(1,128)}), s32[32,1,2]{2,1,0:T(1,128)S(1)}, u32[]{:S(2)}, u32[]{:S(2)}) async-start(s32[32,1,2]{2,1,0:T(1,128)} %bitcast.2), calls=%async_computation | async-start | bytes 32768 | tf_op jit(solution)/shard_map/all_to_all | solution.py:242
  19.6 1.4 copy.25
  21.1 4.8 %all-to-all-done = s32[32,1,2]{2,1,0:T(1,128)S(1)} async-done(((s32[32,1,2]{2,1,0:T(1,128)}), s32[32,1,2]{2,1,0:T(1,128)S(1)}, u32[]{:S(2)}, u32[]{:S(2)}) %all-to-all-start) | async-done | bytes 288 | tf_op jit(solution)/shard_map/all_to_all | solution.py:242
  26.1 9.5 %all-gather.6.cloned.1.call-done = bf16[16,2,128,128]{3,2,1,0:T(8,128)(2,1)} async-done(((bf16[4,2,128,128]{3,2,1,0:T(8,128)(2,1)}), bf16[16,2,128,128]{3,2,1,0:T(8,128)(2,1)}) %all-gather.6.cloned.1.call-update) | async-done | bytes 1048592 | tf_op jit(solution)/shard_map/all_gather | solution.py:266
  35.6 4.2 gather_fusion
  39.9 7.6 %all-to-all-start.1 = ((bf16[64,2,128,128]{3,2,1,0:T(8,128)(2,1)}), bf16[64,2,128,128]{3,2,1,0:T(8,128)(2,1)}, u32[]{:S(2)}, u32[]{:S(2)}) async-start(bf16[64,2,128,128]{3,2,1,0:T(8,128)(2,1)} %gather_fusion), calls=%async_computation.1 | async-start | bytes 8388608 | tf_op jit(solution)/shard_map/all_to_all | solution.py:276
  48.4 32.8 %all-gather.8.cloned.1.call-done = bf16[16,2,128,256]{3,2,1,0:T(8,128)(2,1)} async-done(((bf16[4,2,128,256]{3,2,1,0:T(8,128)(2,1)}), bf16[16,2,128,256]{3,2,1,0:T(8,128)(2,1)}) %all-gather.8.cloned.1.call-update) | async-done | bytes 2097168 | tf_op jit(solution)/shard_map/all_gather | solution.py:266
  81.2 7.0 %gather_fusion.2 = bf16[64,2,128,256]{3,2,1,0:T(8,128)(2,1)} fusion(bf16[16,2,128,256]{3,2,1,0:T(8,128)(2,1)} %all-gather.8.cloned.1.call-done, s32[1024]{0:T(1024)S(1)} %pad_clamp_fusion), kind=kCustom, calls=%fused_computation.2 | custom fusion | bytes 16777472 | tf_op jit(solution)/shard_map/gather | solution.py:276
  88.1 10.4 %all-to-all-done.1.block_ref = bf16[64,2,128,128]{3,2,1,0:T(8,128)(2,1)} async-done(((bf16[64,2,128,128]{3,2,1,0:T(8,128)(2,1)}), bf16[64,2,128,128]{3,2,1,0:T(8,128)(2,1)}, u32[]{:S(2)}, u32[]{:S(2)}) %all-to-all-start.1) | async-done | bytes 4194336 | tf_op jit(solution)/shard_map/all_to_all | solution.py:276
  98.6 7.8 %all-to-all-start.3 = ((bf16[64,2,128,256]{3,2,1,0:T(8,128)(2,1)}), bf16[64,2,128,256]{3,2,1,0:T(8,128)(2,1)}, u32[]{:S(2)}, u32[]{:S(2)}) async-start(bf16[64,2,128,256]{3,2,1,0:T(8,128)(2,1)} %gather_fusion.2), calls=%async_computation.3 | async-start | bytes 16777216 | tf_op jit(solution)/shard_map/all_to_all | solution.py:276
  106.4 1.3 collective-permute-start
  107.7 1.3 collective-permute-start.2
  109.0 129.1 %collective-permute-done.rest_1_ = bf16[2,512,512]{2,1,0:T(8,128)(2,1)S(1)} collective-permute-done((bf16[2,512,512]{2,1,0:T(8,128)(2,1)S(1)}, bf16[2,512,512]{2,1,0:T(8,128)(2,1)S(1)}, u32[]{:S(2)}, u32[]{:S(2)}) %collective-permute-start) | collective-permute-done | bytes 1048608 | tf_op jit(solution)/shard_map/ppermute | solution.py:254
  238.1 1.3 collective-permute-start.1
  239.4 13.1 %collective-permute-done.2.rest_3_ = bf16[2,512,512]{2,1,0:T(8,128)(2,1)S(1)} collective-permute-done((bf16[2,512,512]{2,1,0:T(8,128)(2,1)S(1)}, bf16[2,512,512]{2,1,0:T(8,128)(2,1)S(1)}, u32[]{:S(2)}, u32[]{:S(2)}) %collective-permute-start.2) | collective-permute-done | bytes 1048608 | tf_op jit(solution)/shard_map/ppermute | solution.py:254
  252.5 17.5 %collective-permute-done.1.rest_2_ = bf16[2,512,512]{2,1,0:T(8,128)(2,1)} collective-permute-done((bf16[2,512,512]{2,1,0:T(8,128)(2,1)S(1)}, bf16[2,512,512]{2,1,0:T(8,128)(2,1)}, u32[]{:S(2)}, u32[]{:S(2)}) %collective-permute-start.1) | collective-permute-done | bytes 1048608 | tf_op jit(solution)/shard_map/ppermute | solution.py:254
  270.0 1.5 select_bitcast_fusion.2
  271.6 2.0 pad_maximum_fusion
  273.6 1.5 collective-permute-start.4
  275.3 15.0 %collective-permute-done.4.rest_4_ = bf16[2,512,512]{2,1,0:T(8,128)(2,1)S(1)} collective-permute-done((bf16[2,512,512]{2,1,0:T(8,128)(2,1)S(1)}, bf16[2,512,512]{2,1,0:T(8,128)(2,1)S(1)}, u32[]{:S(2)}, u32[]{:S(2)}) %collective-permute-start.4) | collective-permute-done | bytes 1048608 | tf_op jit(solution)/shard_map/ppermute | solution.py:254
  291.3 32.7 %shard_map.64.state_ref = f32[2,4,640,384]{3,2,1,0:T(8,128)} custom-call(s32[1]{0:T(128)} %bitcast.place_ref, bf16[512,2560]{1,0:T(8,128)(2,1)} %q_ref.11, bf16[2,512,512]{2,1,0:T(8,128)(2,1)} %bitcast.18, bf16[3,2,512,512]{3,2,1,0:T(8,128)(2,1)} %collective-permute-done.3.rest_0_, bf16[2,512,512]{2,1,0:T(8,128)(2,1)} %copy-done.6, ...), custom_call_target="tpu_custom_call" | custom-call | flops 10737418240 | bytes 13369344 | tf_op jit(solution)/shard_map/pallas_call | solution.py:132
  324.0 32.8 %shard_map.65.state_ref = f32[2,4,640,384]{3,2,1,0:T(8,128)} custom-call(s32[1]{0:T(128)} %bitcast.place_ref, bf16[512,2560]{1,0:T(8,128)(2,1)} %q_ref.11, bf16[2,512,512]{2,1,0:T(8,128)(2,1)} %bitcast.19, bf16[3,2,512,512]{3,2,1,0:T(8,128)(2,1)} %collective-permute-done.3.rest_0_, bf16[2,512,512]{2,1,0:T(8,128)(2,1)} %copy-done.6, ...), custom_call_target="tpu_custom_call" | custom-call | flops 10737418240 | bytes 13369344 | tf_op jit(solution)/shard_map/pallas_call | solution.py:132
  356.8 8.3 %shard_map.66.rest_0_ = bf16[512,2560]{1,0:T(8,128)(2,1)} custom-call(s32[4]{0:T(128)S(1)} %copy-done.3, s32[4,8]{1,0:T(4,128)S(1)} %fusion.6.pos_ref, bf16[512,2560]{1,0:T(8,128)(2,1)S(1)} %copy-done, f32[2,4,640,384]{3,2,1,0:T(8,128)} %shard_map.64.state_ref, bf16[64,2,128,128]{3,2,1,0:T(8,128)(2,1)} %all-to-all-done.1.block_ref), custom_call_target="tpu_custom_call" | custom-call | flops 1342177280 | bytes 9437184 | tf_op jit(solution)/shard_map/pallas_call | solution.py:203
  365.1 4.3 gather_fusion.1
  369.3 10.2 %all-to-all-start.2 = ((bf16[64,2,128,128]{3,2,1,0:T(8,128)(2,1)}), bf16[64,2,128,128]{3,2,1,0:T(8,128)(2,1)}, u32[]{:S(2)}, u32[]{:S(2)}) async-start(bf16[64,2,128,128]{3,2,1,0:T(8,128)(2,1)} %gather_fusion.1), calls=%async_computation.2 | async-start | bytes 8388608 | tf_op jit(solution)/shard_map/all_to_all | solution.py:276
  379.5 3.2 copy-done.2
  382.8 7.1 %shard_map.67.rest_0_ = bf16[512,2560]{1,0:T(8,128)(2,1)} custom-call(s32[4]{0:T(128)S(1)} %copy-done.3, s32[4,8]{1,0:T(4,128)S(1)} %fusion.6.pos_ref, bf16[512,2560]{1,0:T(8,128)(2,1)S(1)} %copy-done, f32[2,4,640,384]{3,2,1,0:T(8,128)S(1)} %copy-done.2, bf16[64,2,128,256]{3,2,1,0:T(8,128)(2,1)} %all-to-all-done.3.block_ref, ...), custom_call_target="tpu_custom_call", output_to_operand_aliasing={{}: (5, {})} | custom-call | flops 1342177280 | bytes 13631488 | tf_op jit(solution)/shard_map/pallas_call | solution.py:203
  389.9 3.2 copy-done.1
  393.1 7.1 %shard_map.68.rest_0_ = bf16[512,2560]{1,0:T(8,128)(2,1)} custom-call(s32[4]{0:T(128)S(1)} %copy-done.3, s32[4,8]{1,0:T(4,128)S(1)} %fusion.6.pos_ref, bf16[512,2560]{1,0:T(8,128)(2,1)S(1)} %copy-done, f32[2,4,640,384]{3,2,1,0:T(8,128)S(1)} %copy-done.1, bf16[64,2,128,256]{3,2,1,0:T(8,128)(2,1)} %all-to-all-done.3.block_ref, ...), custom_call_target="tpu_custom_call", output_to_operand_aliasing={{}: (5, {})} | custom-call | flops 1342177280 | bytes 13631488 | tf_op jit(solution)/shard_map/pallas_call | solution.py:203
  400.2 30.1 %all-to-all-done.2.block_ref = bf16[64,2,128,128]{3,2,1,0:T(8,128)(2,1)} async-done(((bf16[64,2,128,128]{3,2,1,0:T(8,128)(2,1)}), bf16[64,2,128,128]{3,2,1,0:T(8,128)(2,1)}, u32[]{:S(2)}, u32[]{:S(2)}) %all-to-all-start.2) | async-done | bytes 4194336 | tf_op jit(solution)/shard_map/all_to_all | solution.py:276
  430.3 8.3 %shard_map.69 = bf16[512,2560]{1,0:T(8,128)(2,1)} custom-call(s32[4]{0:T(128)S(1)} %copy-done.3, s32[4,8]{1,0:T(4,128)S(1)} %fusion.6.pos_ref, bf16[512,2560]{1,0:T(8,128)(2,1)S(1)} %copy-done, f32[2,4,640,384]{3,2,1,0:T(8,128)} %shard_map.65.state_ref, bf16[64,2,128,128]{3,2,1,0:T(8,128)(2,1)} %all-to-all-done.2.block_ref, ...), custom_call_target="tpu_custom_call", output_to_operand_aliasing={{}: (5, {})} | custom-call | flops 1342177280 | bytes 9437184 | tf_op jit(solution)/shard_map/pallas_call | solution.py:203
  (47 shorter events, 6.1 us)
Async XLA Ops:
  6.5 29.1 %all-gather.6.cloned.1.call-start = ((), (), s32[]{:S(2)}) async-start(), calls=%async_computation.5 | async-start | bytes 1310720 | tf_op jit(solution)/shard_map/all_gather | solution.py:266
  12.1 13.7 %all-to-all-start = ((s32[32,1,2]{2,1,0:T(1,128)}), s32[32,1,2]{2,1,0:T(1,128)S(1)}, u32[]{:S(2)}, u32[]{:S(2)}) async-start(s32[32,1,2]{2,1,0:T(1,128)} %bitcast.2), calls=%async_computation | async-start | bytes 32768 | tf_op jit(solution)/shard_map/all_to_all | solution.py:242
  21.1 252.5 %copy-start.4 = (bf16[512,2,512]{2,0,1:T(8,128)(2,1)}, bf16[512,2,512]{2,0,1:T(8,128)(2,1)S(1)}, u32[]{:S(2)}) copy-start(bf16[512,2,512]{2,0,1:T(8,128)(2,1)S(1)} %copy.25) | copy-start | bytes 3145732
  39.9 7.7 %copy-start.5 = (bf16[4,2,128,512]{3,2,1,0:T(8,128)(2,1)S(1)}, bf16[4,2,128,512]{3,2,1,0:T(8,128)(2,1)}, u32[]{:S(2)}) copy-start(bf16[4,2,128,512]{3,2,1,0:T(8,128)(2,1)} %param.8) | copy-start | bytes 3145732
  39.9 58.7 %all-to-all-start.1 = ((bf16[64,2,128,128]{3,2,1,0:T(8,128)(2,1)}), bf16[64,2,128,128]{3,2,1,0:T(8,128)(2,1)}, u32[]{:S(2)}, u32[]{:S(2)}) async-start(bf16[64,2,128,128]{3,2,1,0:T(8,128)(2,1)} %gather_fusion), calls=%async_computation.1 | async-start | bytes 8388608 | tf_op jit(solution)/shard_map/all_to_all | solution.py:276
  47.5 33.7 %all-gather.8.cloned.1.call-start = ((), (), s32[]{:S(2)}) async-start(), calls=%async_computation.6 | async-start | bytes 2621440 | tf_op jit(solution)/shard_map/all_gather | solution.py:266
  98.6 270.7 %all-to-all-start.3 = ((bf16[64,2,128,256]{3,2,1,0:T(8,128)(2,1)}), bf16[64,2,128,256]{3,2,1,0:T(8,128)(2,1)}, u32[]{:S(2)}, u32[]{:S(2)}) async-start(bf16[64,2,128,256]{3,2,1,0:T(8,128)(2,1)} %gather_fusion.2), calls=%async_computation.3 | async-start | bytes 16777216 | tf_op jit(solution)/shard_map/all_to_all | solution.py:276
  106.3 258.7 %all-gather.4.cloned.1.call-start = ((), (), s32[]{:S(2)}) async-start(), calls=%async_computation.4 | async-start | bytes 1310720 | tf_op jit(solution)/shard_map/all_gather | solution.py:266
  106.4 131.7 %collective-permute-start = (bf16[2,512,512]{2,1,0:T(8,128)(2,1)S(1)}, bf16[2,512,512]{2,1,0:T(8,128)(2,1)S(1)}, u32[]{:S(2)}, u32[]{:S(2)}) collective-permute-start(bf16[2,512,512]{2,1,0:T(8,128)(2,1)S(1)} %bitcast.14), channel_id=1, source_target_pairs={{1,3},{2,4},{3,5},{4,6},{5,7},{6,8},{7,9},{9,11},{10,12},{11,13},{... | collective-permute-start | bytes 3145736 | tf_op jit(solution)/shard_map/ppermute | solution.py:254
  107.7 144.8 %collective-permute-start.2 = (bf16[2,512,512]{2,1,0:T(8,128)(2,1)S(1)}, bf16[2,512,512]{2,1,0:T(8,128)(2,1)S(1)}, u32[]{:S(2)}, u32[]{:S(2)}) collective-permute-start(bf16[2,512,512]{2,1,0:T(8,128)(2,1)S(1)} %bitcast.15), channel_id=1, source_target_pairs={{1,7},{2,8},{3,9},{9,15},{10,16},{11,17},{17,23},{18,24},{19,25},{... | collective-permute-start | bytes 3145736 | tf_op jit(solution)/shard_map/ppermute | solution.py:254
  238.1 35.5 %copy-start.6 = (bf16[2,512,512]{2,1,0:T(8,128)(2,1)}, bf16[2,512,512]{2,1,0:T(8,128)(2,1)S(1)}, u32[]{:S(2)}) copy-start(bf16[2,512,512]{2,1,0:T(8,128)(2,1)S(1)} %collective-permute-done.rest_1_) | copy-start | bytes 3145732
  238.1 31.9 %collective-permute-start.1 = (bf16[2,512,512]{2,1,0:T(8,128)(2,1)S(1)}, bf16[2,512,512]{2,1,0:T(8,128)(2,1)}, u32[]{:S(2)}, u32[]{:S(2)}) collective-permute-start(bf16[2,512,512]{2,1,0:T(8,128)(2,1)S(1)} %collective-permute-done.rest_1_), channel_id=1, source_target_pairs={{3,5},{4,6},{5,7},{6,8},{7,9},{11,13},{12,14},{13,15},{14,16},{15,... | collective-permute-start | bytes 3145736 | tf_op jit(solution)/shard_map/ppermute | solution.py:254
  252.5 21.1 %copy-start.7 = (bf16[2,512,512]{2,1,0:T(8,128)(2,1)}, bf16[2,512,512]{2,1,0:T(8,128)(2,1)S(1)}, u32[]{:S(2)}) copy-start(bf16[2,512,512]{2,1,0:T(8,128)(2,1)S(1)} %collective-permute-done.2.rest_3_) | copy-start | bytes 3145732
  271.6 3.7 copy-start.3
  273.6 16.7 %collective-permute-start.3 = (bf16[3,2,512,512]{3,2,1,0:T(8,128)(2,1)}, bf16[3,2,512,512]{3,2,1,0:T(8,128)(2,1)}, u32[]{:S(2)}, u32[]{:S(2)}) collective-permute-start(bf16[3,2,512,512]{3,2,1,0:T(8,128)(2,1)} %pad_maximum_fusion), channel_id=1, source_target_pairs={{0,1},{1,0},{2,3},{3,2},{4,5},{5,4},{6,7},{7,6},{8,9},{9,8},{10,11... | collective-permute-start | bytes 9437192 | tf_op jit(solution)/shard_map/ppermute | solution.py:263
  273.6 16.7 %collective-permute-start.4 = (bf16[2,512,512]{2,1,0:T(8,128)(2,1)S(1)}, bf16[2,512,512]{2,1,0:T(8,128)(2,1)S(1)}, u32[]{:S(2)}, u32[]{:S(2)}) collective-permute-start(bf16[2,512,512]{2,1,0:T(8,128)(2,1)S(1)} %bitcast.17), channel_id=1, source_target_pairs={{1,8},{9,16},{17,24},{25,32},{33,40},{41,48},{49,56},{57,64},{65,7... | collective-permute-start | bytes 3145736 | tf_op jit(solution)/shard_map/ppermute | solution.py:254
  290.3 1.0 copy-start.8
  324.0 32.8 %copy-start = (bf16[512,2560]{1,0:T(8,128)(2,1)S(1)}, bf16[512,2560]{1,0:T(8,128)(2,1)}, u32[]{:S(2)}) copy-start(bf16[512,2560]{1,0:T(8,128)(2,1)} %q_ref.11) | copy-start | bytes 7864324
  369.3 61.0 %all-to-all-start.2 = ((bf16[64,2,128,128]{3,2,1,0:T(8,128)(2,1)}), bf16[64,2,128,128]{3,2,1,0:T(8,128)(2,1)}, u32[]{:S(2)}, u32[]{:S(2)}) async-start(bf16[64,2,128,128]{3,2,1,0:T(8,128)(2,1)} %gather_fusion.1), calls=%async_computation.2 | async-start | bytes 8388608 | tf_op jit(solution)/shard_map/all_to_all | solution.py:276
  379.5 3.2 copy-start.2
  389.9 3.2 copy-start.1
Sparse Core Ops, SparseCore 0:
  9.0 26.6 all-gather.5
  50.0 31.1 all-gather.7
  275.2 25.6 all-gather.3

commit v3 on v2

--- a/solution.py
+++ b/solution.py
@@ -162,24 +162,31 @@
     def listed(t, kind):
         return jnp.concatenate([block_ref[pos_ref[t, i], kind] for i in range(list_len)], axis=0)
 
+    def tile_rows_at(t):
+        return pl.ds(pl.multiple_of(t * tile_rows, tile_rows), tile_rows)
+
     def tile_scores(t):
-        queries = stack_heads(q_ref[t * tile_rows : (t + 1) * tile_rows, :], repeat)
-        return score(queries, listed(t, 0))
-
-    ahead = tile_scores(0)
-    for t in range(tiles):
-        scores = ahead
-        if t + 1 < tiles:
-            ahead = tile_scores(t + 1)
+        return score(stack_heads(q_ref[tile_rows_at(t), :], repeat), listed(t, 0))
+
+    def finish(t, scores):
         masks = [i < count_ref[t] for i in range(list_len)]
         old = [state_ref[0, t, :, i * HEAD : (i + 1) * HEAD] for i in range(3)]
         values_one = jnp.concatenate([listed(t, 1), ones], axis=1)
         _, total, row_sum = weigh(scores, values_one, old[2], old[:2], masks)
         result = (total / row_sum).astype(jnp.bfloat16)
         for r in range(repeat):
-            out_ref[t * tile_rows : (t + 1) * tile_rows, r * HEAD : (r + 1) * HEAD] = result[
+            out_ref[tile_rows_at(t), r * HEAD : (r + 1) * HEAD] = result[
                 r * tile_rows : (r + 1) * tile_rows, :
             ]
+
+    def pair(i, carry):
+        first = tile_scores(2 * i)
+        second = tile_scores(2 * i + 1)
+        finish(2 * i, first)
+        finish(2 * i + 1, second)
+        return carry
+
+    lax.fori_loop(0, tiles // 2, pair, 0)
 
 
 def listed_attention(head, state_row, counts, position, queries, state, blocks, lane, partial_out):
@@ -220,7 +227,7 @@
 
 
 def local(summary_q, summary_kv, kv_cache, block_slot, tile_blocks, tile_count):
-    plane, devices = lax.axis_size(PLANE), lax.axis_size(ALL)
+    plane, groups, devices = (lax.axis_size(axes) for axes in (PLANE, "z", ALL))
     tile_num, list_len = tile_blocks.shape
     blk_dev = kv_cache.shape[0]
     req_devs = REQ_TILES // tile_num
@@ -240,6 +247,8 @@
         owner_dev // plane * blk_dev + stored_at % blk_dev,
     )
     asked = lax.all_to_all(requests, PLANE, split_axis=0, concat_axis=0, tiled=True)
+    depth = (lax.axis_index("z") - asked // blk_dev + groups) % groups
+    asked = depth * blk_dev + asked % blk_dev
     position = jnp.where(live_mask, position, 0).reshape(tile_num, list_len)
     place = (flat_index - 1 + req_devs) % req_devs
     own, asked = lax.optimization_barrier((summary_kv.transpose(1, 0, 2), asked))
@@ -262,12 +271,16 @@
     give = [jnp.where(core == 0, a, b) for a, b in zip([own, *same[:-1]], same, strict=True)]
     other = lax.ppermute(jnp.stack(give), "c", [(0, 1), (1, 0)])
     earlier = [other, *same, first]
-    columns = [
-        lax.all_gather(
-            kv_cache[..., heads[0] * HEAD : (heads[-1] + 1) * HEAD], "z", axis=0, tiled=True
-        )
-        for heads in CHUNKS
-    ]
+
+    def stack_column(heads):
+        part = kv_cache[..., heads[0] * HEAD : (heads[-1] + 1) * HEAD]
+        pieces = [part]
+        for step in range(1, groups):
+            pairs = [(source, (source + step) % groups) for source in range(groups)]
+            pieces.append(lax.ppermute(part, "z", pairs))
+        return jnp.concatenate(pieces, axis=0)
+
+    columns = [stack_column(heads) for heads in CHUNKS]
     states, received, out = [], {}, None
     for turn, heads in enumerate(CHUNKS):
         column = columns[turn]

time: 449 us -> 438 us (0.976)
  starting transfers between devices: 38.5 us -> 58.9 us
  waiting for transfers between devices: 262 us -> 247 us
  between operations: 13.3 us -> 0.27 us
  local copies, waits for them, and re-layouts: 29.1 us -> 23.4 us
    all_gather x3 -> x0, waiting for transfers between devices: 42.3 us -> none  [local(): lax.all_gather(kv_cache[..., heads[0] * HEAD:(heads[-1] + 1) * HEAD], 'z'...]
    ppermute x0 -> x9, waiting for transfers between devices: none -> 37.8 us  [stack_column(): pieces.append(lax.ppermute(part, 'z', pairs))]
    ppermute x4, waiting for transfers between devices: 175 us -> 159 us  [ahead(): return lax.ppermute(value, ALL, pairs)]
    ppermute x0 -> x9, starting transfers between devices: none -> 14.1 us  [stack_column(): pieces.append(lax.ppermute(part, 'z', pairs))]
    all_to_all x3, starting transfers between devices: 25.5 us -> 32.2 us  [local(): lax.all_to_all(column[asked], PLANE, split_axis=0, concat_axis=0, tiled=T...]
    all_to_all x3, waiting for transfers between devices: 40.6 us -> 46.1 us  [local(): lax.all_to_all(column[asked], PLANE, split_axis=0, concat_axis=0, tiled=T...]
  transfers between devices with their start and end apart: 12 -> 18, of which waited for: 9 -> 12; matrix products, arithmetic and copies ran while one was open for 5% -> 4% of each run, Pallas kernels for 20% -> 21%
where the time goes in v3:
time: 438 us; the launch traced here: 434 us
  waiting for transfers between devices  247 us (56%)
  Pallas kernels  97.9 us (22%)
  starting transfers between devices  58.9 us (13%)
  local copies, waits for them, and re-layouts  23.4 us (5%)
  other arithmetic  6.49 us (1%)
    ppermute x4, waiting for transfers between devices, ahead(): return lax.ppermute(value, ALL, pairs)  159 us
    pallas_call x2, Pallas kernels, span_attention(): pl.pallas_call(functools.partial(span_kernel, repeat, tile_rows), out_sha...  65.5 us
    all_to_all x3, waiting for transfers between devices, local(): lax.all_to_all(column[asked], PLANE, split_axis=0, concat_axis=0, tiled=T...  46.1 us
    ppermute x9, waiting for transfers between devices, stack_column(): pieces.append(lax.ppermute(part, 'z', pairs))  37.8 us
    pallas_call x4, Pallas kernels, listed_attention(): pl.pallas_call(functools.partial(listed_kernel, repeat, tile_rows), out_s...  32.4 us
    all_to_all x3, starting transfers between devices, local(): lax.all_to_all(column[asked], PLANE, split_axis=0, concat_axis=0, tiled=T...  32.2 us
    ppermute x9, starting transfers between devices, stack_column(): pieces.append(lax.ppermute(part, 'z', pairs))  14.1 us
    gather x3, local copies, waits for them, and re-layouts, local(): column[asked]  11.5 us
  transfers between devices with their start and end apart: 18, of which 12 were waited for; matrix products, arithmetic and copies ran while one was open for 4% of the time, Pallas kernels for 21%

profile of v3, /device:TPU:8, one launch (start us, length us, event | category | flops | bytes accessed | tf_op | source)
XLA Modules:
  0.0 434.4 jit_solution(10473454507029885355)
XLA Ops:
  1.1 4.1 collective-permute-start.10
  10.1 7.5 %all-to-all-start = ((s32[32,1,2]{2,1,0:T(1,128)}), s32[32,1,2]{2,1,0:T(1,128)S(1)}, u32[]{:S(2)}, u32[]{:S(2)}) async-start(s32[32,1,2]{2,1,0:T(1,128)} %bitcast.2), calls=%async_computation | async-start | bytes 32768 | tf_op jit(solution)/shard_map/all_to_all | solution.py:249
  19.0 4.7 %all-to-all-done = s32[32,1,2]{2,1,0:T(1,128)S(1)} async-done(((s32[32,1,2]{2,1,0:T(1,128)}), s32[32,1,2]{2,1,0:T(1,128)S(1)}, u32[]{:S(2)}, u32[]{:S(2)}) %all-to-all-start) | async-done | bytes 288 | tf_op jit(solution)/shard_map/all_to_all | solution.py:249
  24.3 3.0 gather_fusion
  27.3 6.0 %all-to-all-start.1 = ((bf16[64,2,128,128]{3,2,1,0:T(8,128)(2,1)}), bf16[64,2,128,128]{3,2,1,0:T(8,128)(2,1)}, u32[]{:S(2)}, u32[]{:S(2)}) async-start(bf16[64,2,128,128]{3,2,1,0:T(8,128)(2,1)} %gather_fusion), calls=%async_computation.1 | async-start | bytes 8388608 | tf_op jit(solution)/shard_map/all_to_all | solution.py:289
  33.4 2.0 collective-permute-start.13
  35.4 2.3 collective-permute-start.12
  37.7 10.7 %collective-permute-done.13 = bf16[4,2,128,256]{3,2,1,0:T(8,128)(2,1)S(1)} collective-permute-done((bf16[4,2,128,256]{3,2,1,0:T(8,128)(2,1)S(1)}, bf16[4,2,128,256]{3,2,1,0:T(8,128)(2,1)S(1)}, u32[]{:S(2)}, u32[]{:S(2)}) %collective-permute-start.13) | collective-permute-done | bytes 524320 | tf_op jit(solution)/shard_map/ppermute | solution.py:280
  48.5 3.3 collective-permute-done.12
  51.8 10.1 %collective-permute-done.11 = bf16[4,2,128,256]{3,2,1,0:T(8,128)(2,1)S(1)} collective-permute-done((bf16[4,2,128,256]{3,2,1,0:T(8,128)(2,1)S(1)}, bf16[4,2,128,256]{3,2,1,0:T(8,128)(2,1)S(1)}, u32[]{:S(2)}, u32[]{:S(2)}) %collective-permute-start.11) | collective-permute-done | bytes 524320 | tf_op jit(solution)/shard_map/ppermute | solution.py:280
  62.1 5.4 %gather_fusion.2 = bf16[64,2,128,256]{3,2,1,0:T(8,128)(2,1)} fusion(bf16[16,2,128,256]{3,2,1,0:T(8,128)(2,1)S(1)} %pad_maximum_fusion.1, s32[1024]{0:T(1024)S(1)} %pad_clamp_fusion), kind=kCustom, calls=%fused_computation.2 | custom fusion | bytes 16777472 | tf_op jit(solution)/shard_map/gather | solution.py:289
  67.5 16.7 %all-to-all-done.1.block_ref = bf16[64,2,128,128]{3,2,1,0:T(8,128)(2,1)} async-done(((bf16[64,2,128,128]{3,2,1,0:T(8,128)(2,1)}), bf16[64,2,128,128]{3,2,1,0:T(8,128)(2,1)}, u32[]{:S(2)}, u32[]{:S(2)}) %all-to-all-start.1) | async-done | bytes 4194336 | tf_op jit(solution)/shard_map/all_to_all | solution.py:289
  84.2 8.0 %all-to-all-start.3 = ((bf16[64,2,128,256]{3,2,1,0:T(8,128)(2,1)}), bf16[64,2,128,256]{3,2,1,0:T(8,128)(2,1)}, u32[]{:S(2)}, u32[]{:S(2)}) async-start(bf16[64,2,128,256]{3,2,1,0:T(8,128)(2,1)} %gather_fusion.2), calls=%async_computation.3 | async-start | bytes 16777216 | tf_op jit(solution)/shard_map/all_to_all | solution.py:289
  94.9 129.2 %collective-permute-done.3.rest_1_ = bf16[2,512,512]{2,1,0:T(8,128)(2,1)} collective-permute-done((bf16[2,512,512]{2,1,0:T(8,128)(2,1)S(1)}, bf16[2,512,512]{2,1,0:T(8,128)(2,1)}, u32[]{:S(2)}, u32[]{:S(2)}) %collective-permute-start.3) | collective-permute-done | bytes 1048608 | tf_op jit(solution)/shard_map/ppermute | solution.py:263
  225.4 12.5 %collective-permute-done.5.rest_3_ = bf16[2,512,512]{2,1,0:T(8,128)(2,1)S(1)} collective-permute-done((bf16[2,512,512]{2,1,0:T(8,128)(2,1)S(1)}, bf16[2,512,512]{2,1,0:T(8,128)(2,1)S(1)}, u32[]{:S(2)}, u32[]{:S(2)}) %collective-permute-start.5) | collective-permute-done | bytes 1048608 | tf_op jit(solution)/shard_map/ppermute | solution.py:263
  238.9 17.1 %collective-permute-done.4.rest_2_ = bf16[2,512,512]{2,1,0:T(8,128)(2,1)} collective-permute-done((bf16[2,512,512]{2,1,0:T(8,128)(2,1)}, bf16[2,512,512]{2,1,0:T(8,128)(2,1)}, u32[]{:S(2)}, u32[]{:S(2)}) %collective-permute-start.4) | collective-permute-done | bytes 1048608 | tf_op jit(solution)/shard_map/ppermute | solution.py:263
  261.1 2.0 collective-permute-start.2
  263.1 2.3 collective-permute-start.1
  265.7 4.1 collective-permute-done.2
  269.8 3.9 collective-permute-done.1
  273.7 5.7 %collective-permute-done = bf16[4,2,128,128]{3,2,1,0:T(8,128)(2,1)S(1)} collective-permute-done((bf16[4,2,128,128]{3,2,1,0:T(8,128)(2,1)S(1)}, bf16[4,2,128,128]{3,2,1,0:T(8,128)(2,1)S(1)}, u32[]{:S(2)}, u32[]{:S(2)}) %collective-permute-start) | collective-permute-done | bytes 262176 | tf_op jit(solution)/shard_map/ppermute | solution.py:280
  279.6 32.8 %shard_map.64.state_ref = f32[2,4,640,384]{3,2,1,0:T(8,128)} custom-call(s32[1]{0:T(128)} %bitcast.place_ref, bf16[512,2560]{1,0:T(8,128)(2,1)} %q_ref.11, bf16[2,512,512]{2,1,0:T(8,128)(2,1)} %bitcast.31, bf16[3,2,512,512]{3,2,1,0:T(8,128)(2,1)} %collective-permute-done.6.rest_0_, bf16[2,512,512]{2,1,0:T(8,128)(2,1)} %collective-permute-done.3.rest_1_, ...), custom_call_target="tpu_custom_call" | custom-call | flops 10737418240 | bytes 13369344 | tf_op jit(solution)/shard_map/pallas_call | solution.py:132
  312.4 8.7 %shard_map.66.rest_0_ = bf16[512,2560]{1,0:T(8,128)(2,1)} custom-call(s32[4]{0:T(128)S(1)} %copy-done.4, s32[4,8]{1,0:T(4,128)S(1)} %fusion.6.pos_ref, bf16[512,2560]{1,0:T(8,128)(2,1)S(1)} %copy-done, f32[2,4,640,384]{3,2,1,0:T(8,128)} %shard_map.64.state_ref, bf16[64,2,128,128]{3,2,1,0:T(8,128)(2,1)} %all-to-all-done.1.block_ref), custom_call_target="tpu_custom_call" | custom-call | flops 1342177280 | bytes 9437184 | tf_op jit(solution)/shard_map/pallas_call | solution.py:210
  321.1 32.6 %shard_map.65.state_ref = f32[2,4,640,384]{3,2,1,0:T(8,128)} custom-call(s32[1]{0:T(128)} %bitcast.place_ref, bf16[512,2560]{1,0:T(8,128)(2,1)} %q_ref.11, bf16[2,512,512]{2,1,0:T(8,128)(2,1)} %bitcast.32, bf16[3,2,512,512]{3,2,1,0:T(8,128)(2,1)} %collective-permute-done.6.rest_0_, bf16[2,512,512]{2,1,0:T(8,128)(2,1)} %collective-permute-done.3.rest_1_, ...), custom_call_target="tpu_custom_call" | custom-call | flops 10737418240 | bytes 13369344 | tf_op jit(solution)/shard_map/pallas_call | solution.py:132
  353.8 3.0 gather_fusion.1
  356.8 18.1 %all-to-all-start.2 = ((bf16[64,2,128,128]{3,2,1,0:T(8,128)(2,1)}), bf16[64,2,128,128]{3,2,1,0:T(8,128)(2,1)}, u32[]{:S(2)}, u32[]{:S(2)}) async-start(bf16[64,2,128,128]{3,2,1,0:T(8,128)(2,1)} %gather_fusion.1), calls=%async_computation.2 | async-start | bytes 8388608 | tf_op jit(solution)/shard_map/all_to_all | solution.py:289
  375.0 3.2 copy-done.3
  378.2 7.5 %shard_map.67.rest_0_ = bf16[512,2560]{1,0:T(8,128)(2,1)} custom-call(s32[4]{0:T(128)S(1)} %copy-done.4, s32[4,8]{1,0:T(4,128)S(1)} %fusion.6.pos_ref, bf16[512,2560]{1,0:T(8,128)(2,1)S(1)} %copy-done.1, f32[2,4,640,384]{3,2,1,0:T(8,128)S(1)} %copy-done.3, bf16[64,2,128,256]{3,2,1,0:T(8,128)(2,1)} %all-to-all-done.3.block_ref, ...), custom_call_target="tpu_custom_call", output_to_operand_aliasing={{}: (5, {})} | custom-call | flops 1342177280 | bytes 13631488 | tf_op jit(solution)/shard_map/pallas_call | solution.py:210
  385.7 3.2 copy-done.2
  388.9 7.5 %shard_map.68.rest_0_ = bf16[512,2560]{1,0:T(8,128)(2,1)} custom-call(s32[4]{0:T(128)S(1)} %copy-done.4, s32[4,8]{1,0:T(4,128)S(1)} %fusion.6.pos_ref, bf16[512,2560]{1,0:T(8,128)(2,1)S(1)} %copy-done.1, f32[2,4,640,384]{3,2,1,0:T(8,128)S(1)} %copy-done.2, bf16[64,2,128,256]{3,2,1,0:T(8,128)(2,1)} %all-to-all-done.3.block_ref, ...), custom_call_target="tpu_custom_call", output_to_operand_aliasing={{}: (5, {})} | custom-call | flops 1342177280 | bytes 13631488 | tf_op jit(solution)/shard_map/pallas_call | solution.py:210
  396.4 29.3 %all-to-all-done.2.block_ref = bf16[64,2,128,128]{3,2,1,0:T(8,128)(2,1)} async-done(((bf16[64,2,128,128]{3,2,1,0:T(8,128)(2,1)}), bf16[64,2,128,128]{3,2,1,0:T(8,128)(2,1)}, u32[]{:S(2)}, u32[]{:S(2)}) %all-to-all-start.2) | async-done | bytes 4194336 | tf_op jit(solution)/shard_map/all_to_all | solution.py:289
  425.7 8.7 %shard_map.69 = bf16[512,2560]{1,0:T(8,128)(2,1)} custom-call(s32[4]{0:T(128)S(1)} %copy-done.4, s32[4,8]{1,0:T(4,128)S(1)} %fusion.6.pos_ref, bf16[512,2560]{1,0:T(8,128)(2,1)S(1)} %copy-done.1, f32[2,4,640,384]{3,2,1,0:T(8,128)} %shard_map.65.state_ref, bf16[64,2,128,128]{3,2,1,0:T(8,128)(2,1)} %all-to-all-done.2.block_ref, ...), custom_call_target="tpu_custom_call", output_to_operand_aliasing={{}: (5, {})} | custom-call | flops 1342177280 | bytes 9437184 | tf_op jit(solution)/shard_map/pallas_call | solution.py:210
  (58 shorter events, 18.4 us)
Async XLA Ops:
  1.1 23.0 %collective-permute-start.10 = (bf16[4,2,128,128]{3,2,1,0:T(8,128)(2,1)S(1)}, bf16[4,2,128,128]{3,2,1,0:T(8,128)(2,1)S(1)}, u32[]{:S(2)}, u32[]{:S(2)}) collective-permute-start(bf16[4,2,128,128]{3,2,1,0:T(8,128)(2,1)S(1)} %get-tuple-element.19), channel_id=1, source_target_pairs={{0,96},{32,0},{64,32},{96,64},{1,97},{33,1},{65,33},{97,65},{2,98}... | collective-permute-start | bytes 786440 | tf_op jit(solution)/shard_map/ppermute | solution.py:280
  5.2 18.9 %collective-permute-start.9 = (bf16[4,2,128,128]{3,2,1,0:T(8,128)(2,1)S(1)}, bf16[4,2,128,128]{3,2,1,0:T(8,128)(2,1)S(1)}, u32[]{:S(2)}, u32[]{:S(2)}) collective-permute-start(bf16[4,2,128,128]{3,2,1,0:T(8,128)(2,1)S(1)} %get-tuple-element.19), channel_id=1, source_target_pairs={{0,64},{32,96},{64,0},{96,32},{1,65},{33,97},{65,1},{97,33},{2,66}... | collective-permute-start | bytes 786440 | tf_op jit(solution)/shard_map/ppermute | solution.py:280
  5.2 18.9 %collective-permute-start.8 = (bf16[4,2,128,128]{3,2,1,0:T(8,128)(2,1)S(1)}, bf16[4,2,128,128]{3,2,1,0:T(8,128)(2,1)S(1)}, u32[]{:S(2)}, u32[]{:S(2)}) collective-permute-start(bf16[4,2,128,128]{3,2,1,0:T(8,128)(2,1)S(1)} %get-tuple-element.19), channel_id=1, source_target_pairs={{0,32},{32,64},{64,96},{96,0},{1,33},{33,65},{65,97},{97,1},{2,34}... | collective-permute-start | bytes 786440 | tf_op jit(solution)/shard_map/ppermute | solution.py:280
  10.1 13.7 %all-to-all-start = ((s32[32,1,2]{2,1,0:T(1,128)}), s32[32,1,2]{2,1,0:T(1,128)S(1)}, u32[]{:S(2)}, u32[]{:S(2)}) async-start(s32[32,1,2]{2,1,0:T(1,128)} %bitcast.2), calls=%async_computation | async-start | bytes 32768 | tf_op jit(solution)/shard_map/all_to_all | solution.py:249
  19.0 240.7 %copy-start.5 = (bf16[512,2,512]{2,0,1:T(8,128)(2,1)}, bf16[512,2,512]{2,0,1:T(8,128)(2,1)S(1)}, u32[]{:S(2)}) copy-start(bf16[512,2,512]{2,0,1:T(8,128)(2,1)S(1)} %copy.25) | copy-start | bytes 3145732
  27.3 6.0 %copy-start.6 = (bf16[4,2,128,512]{3,2,1,0:T(8,128)(2,1)S(1)}, bf16[4,2,128,512]{3,2,1,0:T(8,128)(2,1)}, u32[]{:S(2)}) copy-start(bf16[4,2,128,512]{3,2,1,0:T(8,128)(2,1)} %param.8) | copy-start | bytes 3145732
  27.3 56.9 %all-to-all-start.1 = ((bf16[64,2,128,128]{3,2,1,0:T(8,128)(2,1)}), bf16[64,2,128,128]{3,2,1,0:T(8,128)(2,1)}, u32[]{:S(2)}, u32[]{:S(2)}) async-start(bf16[64,2,128,128]{3,2,1,0:T(8,128)(2,1)} %gather_fusion), calls=%async_computation.1 | async-start | bytes 8388608 | tf_op jit(solution)/shard_map/all_to_all | solution.py:289
  33.4 15.1 %collective-permute-start.13 = (bf16[4,2,128,256]{3,2,1,0:T(8,128)(2,1)S(1)}, bf16[4,2,128,256]{3,2,1,0:T(8,128)(2,1)S(1)}, u32[]{:S(2)}, u32[]{:S(2)}) collective-permute-start(bf16[4,2,128,256]{3,2,1,0:T(8,128)(2,1)S(1)} %slice.11), channel_id=1, source_target_pairs={{0,96},{32,0},{64,32},{96,64},{1,97},{33,1},{65,33},{97,65},{2,98}... | collective-permute-start | bytes 1572872 | tf_op jit(solution)/shard_map/ppermute | solution.py:280
  35.4 16.3 %collective-permute-start.12 = (bf16[4,2,128,256]{3,2,1,0:T(8,128)(2,1)S(1)}, bf16[4,2,128,256]{3,2,1,0:T(8,128)(2,1)S(1)}, u32[]{:S(2)}, u32[]{:S(2)}) collective-permute-start(bf16[4,2,128,256]{3,2,1,0:T(8,128)(2,1)S(1)} %slice.11), channel_id=1, source_target_pairs={{0,64},{32,96},{64,0},{96,32},{1,65},{33,97},{65,1},{97,33},{2,66}... | collective-permute-start | bytes 1572872 | tf_op jit(solution)/shard_map/ppermute | solution.py:280
  37.7 24.1 %collective-permute-start.11 = (bf16[4,2,128,256]{3,2,1,0:T(8,128)(2,1)S(1)}, bf16[4,2,128,256]{3,2,1,0:T(8,128)(2,1)S(1)}, u32[]{:S(2)}, u32[]{:S(2)}) collective-permute-start(bf16[4,2,128,256]{3,2,1,0:T(8,128)(2,1)S(1)} %slice.11), channel_id=1, source_target_pairs={{0,32},{32,64},{64,96},{96,0},{1,33},{33,65},{65,97},{97,1},{2,34}... | collective-permute-start | bytes 1572872 | tf_op jit(solution)/shard_map/ppermute | solution.py:280
  84.2 272.6 %all-to-all-start.3 = ((bf16[64,2,128,256]{3,2,1,0:T(8,128)(2,1)}), bf16[64,2,128,256]{3,2,1,0:T(8,128)(2,1)}, u32[]{:S(2)}, u32[]{:S(2)}) async-start(bf16[64,2,128,256]{3,2,1,0:T(8,128)(2,1)} %gather_fusion.2), calls=%async_computation.3 | async-start | bytes 16777216 | tf_op jit(solution)/shard_map/all_to_all | solution.py:289
  92.3 131.8 %collective-permute-start.3 = (bf16[2,512,512]{2,1,0:T(8,128)(2,1)S(1)}, bf16[2,512,512]{2,1,0:T(8,128)(2,1)}, u32[]{:S(2)}, u32[]{:S(2)}) collective-permute-start(bf16[2,512,512]{2,1,0:T(8,128)(2,1)S(1)} %bitcast.27), channel_id=1, source_target_pairs={{1,3},{2,4},{3,5},{4,6},{5,7},{6,8},{7,9},{9,11},{10,12},{11,13},{... | collective-permute-start | bytes 3145736 | tf_op jit(solution)/shard_map/ppermute | solution.py:263
  93.6 144.3 %collective-permute-start.5 = (bf16[2,512,512]{2,1,0:T(8,128)(2,1)S(1)}, bf16[2,512,512]{2,1,0:T(8,128)(2,1)S(1)}, u32[]{:S(2)}, u32[]{:S(2)}) collective-permute-start(bf16[2,512,512]{2,1,0:T(8,128)(2,1)S(1)} %bitcast.28), channel_id=1, source_target_pairs={{1,7},{2,8},{3,9},{9,15},{10,16},{11,17},{17,23},{18,24},{19,25},{... | collective-permute-start | bytes 3145736 | tf_op jit(solution)/shard_map/ppermute | solution.py:263
  224.1 31.8 %collective-permute-start.4 = (bf16[2,512,512]{2,1,0:T(8,128)(2,1)}, bf16[2,512,512]{2,1,0:T(8,128)(2,1)}, u32[]{:S(2)}, u32[]{:S(2)}) collective-permute-start(bf16[2,512,512]{2,1,0:T(8,128)(2,1)} %collective-permute-done.3.rest_1_), channel_id=1, source_target_pairs={{3,5},{4,6},{5,7},{6,8},{7,9},{11,13},{12,14},{13,15},{14,16},{15,... | collective-permute-start | bytes 3145736 | tf_op jit(solution)/shard_map/ppermute | solution.py:263
  237.9 1.0 copy-start.7
  257.7 7.9 %copy-start.4 = (s32[4]{0:T(128)S(1)}, s32[4]{0:T(128)}, u32[]{:S(2)}) copy-start(s32[4]{0:T(128)} %count_ref.7) | copy-start | bytes 52
  259.8 19.8 %collective-permute-start.6 = (bf16[3,2,512,512]{3,2,1,0:T(8,128)(2,1)}, bf16[3,2,512,512]{3,2,1,0:T(8,128)(2,1)}, u32[]{:S(2)}, u32[]{:S(2)}) collective-permute-start(bf16[3,2,512,512]{3,2,1,0:T(8,128)(2,1)} %pad_maximum_fusion), channel_id=1, source_target_pairs={{0,1},{1,0},{2,3},{3,2},{4,5},{5,4},{6,7},{7,6},{8,9},{9,8},{10,11... | collective-permute-start | bytes 9437192 | tf_op jit(solution)/shard_map/ppermute | solution.py:272
  259.8 19.8 %collective-permute-start.7 = (bf16[2,512,512]{2,1,0:T(8,128)(2,1)S(1)}, bf16[2,512,512]{2,1,0:T(8,128)(2,1)}, u32[]{:S(2)}, u32[]{:S(2)}) collective-permute-start(bf16[2,512,512]{2,1,0:T(8,128)(2,1)S(1)} %bitcast.30), channel_id=1, source_target_pairs={{1,8},{9,16},{17,24},{25,32},{33,40},{41,48},{49,56},{57,64},{65,7... | collective-permute-start | bytes 3145736 | tf_op jit(solution)/shard_map/ppermute | solution.py:263
  261.1 8.7 %collective-permute-start.2 = (bf16[4,2,128,128]{3,2,1,0:T(8,128)(2,1)S(1)}, bf16[4,2,128,128]{3,2,1,0:T(8,128)(2,1)S(1)}, u32[]{:S(2)}, u32[]{:S(2)}) collective-permute-start(bf16[4,2,128,128]{3,2,1,0:T(8,128)(2,1)S(1)} %get-tuple-element.20), channel_id=1, source_target_pairs={{0,96},{32,0},{64,32},{96,64},{1,97},{33,1},{65,33},{97,65},{2,98}... | collective-permute-start | bytes 786440 | tf_op jit(solution)/shard_map/ppermute | solution.py:280
  263.1 10.6 %collective-permute-start.1 = (bf16[4,2,128,128]{3,2,1,0:T(8,128)(2,1)S(1)}, bf16[4,2,128,128]{3,2,1,0:T(8,128)(2,1)S(1)}, u32[]{:S(2)}, u32[]{:S(2)}) collective-permute-start(bf16[4,2,128,128]{3,2,1,0:T(8,128)(2,1)S(1)} %get-tuple-element.20), channel_id=1, source_target_pairs={{0,64},{32,96},{64,0},{96,32},{1,65},{33,97},{65,1},{97,33},{2,66}... | collective-permute-start | bytes 786440 | tf_op jit(solution)/shard_map/ppermute | solution.py:280
  265.4 14.0 %collective-permute-start = (bf16[4,2,128,128]{3,2,1,0:T(8,128)(2,1)S(1)}, bf16[4,2,128,128]{3,2,1,0:T(8,128)(2,1)S(1)}, u32[]{:S(2)}, u32[]{:S(2)}) collective-permute-start(bf16[4,2,128,128]{3,2,1,0:T(8,128)(2,1)S(1)} %get-tuple-element.20), channel_id=1, source_target_pairs={{0,32},{32,64},{64,96},{96,0},{1,33},{33,65},{65,97},{97,1},{2,34}... | collective-permute-start | bytes 786440 | tf_op jit(solution)/shard_map/ppermute | solution.py:280
  279.6 32.8 %copy-start = (bf16[512,2560]{1,0:T(8,128)(2,1)S(1)}, bf16[512,2560]{1,0:T(8,128)(2,1)}, u32[]{:S(2)}) copy-start(bf16[512,2560]{1,0:T(8,128)(2,1)} %q_ref.11) | copy-start | bytes 7864324
  356.8 18.1 %copy-start.1 = (bf16[512,2560]{1,0:T(8,128)(2,1)S(1)}, bf16[512,2560]{1,0:T(8,128)(2,1)}, u32[]{:S(2)}) copy-start(bf16[512,2560]{1,0:T(8,128)(2,1)} %q_ref.11) | copy-start | bytes 7864324
  356.8 68.9 %all-to-all-start.2 = ((bf16[64,2,128,128]{3,2,1,0:T(8,128)(2,1)}), bf16[64,2,128,128]{3,2,1,0:T(8,128)(2,1)}, u32[]{:S(2)}, u32[]{:S(2)}) async-start(bf16[64,2,128,128]{3,2,1,0:T(8,128)(2,1)} %gather_fusion.1), calls=%async_computation.2 | async-start | bytes 8388608 | tf_op jit(solution)/shard_map/all_to_all | solution.py:289
  374.9 3.2 copy-start.3
  385.7 3.2 copy-start.2

commit v4 on v3

--- a/solution.py
+++ b/solution.py
@@ -263,10 +263,13 @@
         return lax.ppermute(value, ALL, pairs)
 
     core = lax.axis_index("c")
-    second = ahead(own, 2, lambda p: p + 2 <= req_devs)
+    near = ahead(own, 2, lambda p: p + 2 < req_devs - 1)
+    lifted = ahead(own, req_devs, lambda p: req_devs - 3 <= p <= req_devs - 2)
+    fallen = ahead(lifted, 2 - req_devs, lambda p: req_devs - 3 <= p <= req_devs - 2)
+    second = near + fallen
     sixth = ahead(own, 6, lambda p: p + 6 <= req_devs)
     first = ahead(own, req_devs - 1, lambda p: p == 0)
-    fourth = ahead(second, 2, lambda p: 2 <= p <= req_devs - 2)
+    fourth = ahead(near, 2, lambda p: 2 <= p <= req_devs - 2)
     same = [second, fourth, sixth]
     give = [jnp.where(core == 0, a, b) for a, b in zip([own, *same[:-1]], same, strict=True)]
     other = lax.ppermute(jnp.stack(give), "c", [(0, 1), (1, 0)])
@@ -278,7 +281,7 @@
         for step in range(1, groups):
             pairs = [(source, (source + step) % groups) for source in range(groups)]
             pieces.append(lax.ppermute(part, "z", pairs))
-        return jnp.concatenate(pieces, axis=0)
+        return pieces
 
     columns = [stack_column(heads) for heads in CHUNKS]
     states, received, out = [], {}, None
@@ -286,6 +289,7 @@
         column = columns[turn]
         if turn > 0:
             column, states, out = lax.optimization_barrier((column, states, out))
+        column = jnp.concatenate(column, axis=0)
         arrived = lax.all_to_all(column[asked], PLANE, split_axis=0, concat_axis=0, tiled=True)
         for i, head in enumerate(heads):
             received[head] = (arrived, i)

time: 438 us -> 422 us (0.963)
  waiting for transfers between devices: 247 us -> 230 us
    ppermute x9, waiting for transfers between devices: 37.8 us -> 22.4 us  [stack_column(): pieces.append(lax.ppermute(part, 'z', pairs))]
    all_to_all x3, starting transfers between devices: 32.2 us -> 25 us  [local(): lax.all_to_all(column[asked], PLANE, split_axis=0, concat_axis=0, tiled=T...]
    ppermute x4 -> x6, waiting for transfers between devices: 159 us -> 157 us  [ahead(): return lax.ppermute(value, ALL, pairs)]
  transfers between devices with their start and end apart: 18 -> 20, of which waited for: 12 -> 10; matrix products, arithmetic and copies ran while one was open for 4% -> 5% of each run, Pallas kernels for 21% -> 21%
where the time goes in v4:
time: 422 us; the launch traced here: 418 us
  waiting for transfers between devices  230 us (55%)
  Pallas kernels  97.9 us (23%)
  starting transfers between devices  55.1 us (13%)
  local copies, waits for them, and re-layouts  24.7 us (6%)
  other arithmetic  9.95 us (2%)
    ppermute x6, waiting for transfers between devices, ahead(): return lax.ppermute(value, ALL, pairs)  157 us
    pallas_call x2, Pallas kernels, span_attention(): pl.pallas_call(functools.partial(span_kernel, repeat, tile_rows), out_sha...  65.5 us
    all_to_all x3, waiting for transfers between devices, local(): lax.all_to_all(column[asked], PLANE, split_axis=0, concat_axis=0, tiled=T...  46.2 us
    pallas_call x4, Pallas kernels, listed_attention(): pl.pallas_call(functools.partial(listed_kernel, repeat, tile_rows), out_s...  32.4 us
    all_to_all x3, starting transfers between devices, local(): lax.all_to_all(column[asked], PLANE, split_axis=0, concat_axis=0, tiled=T...  25 us
    ppermute x9, waiting for transfers between devices, stack_column(): pieces.append(lax.ppermute(part, 'z', pairs))  22.4 us
    ppermute x9, starting transfers between devices, stack_column(): pieces.append(lax.ppermute(part, 'z', pairs))  14.1 us
    gather x3, local copies, waits for them, and re-layouts, local(): column[asked]  12.7 us
  transfers between devices with their start and end apart: 20, of which 10 were waited for; matrix products, arithmetic and copies ran while one was open for 5% of the time, Pallas kernels for 21%

profile of v4, /device:TPU:8, one launch (start us, length us, event | category | flops | bytes accessed | tf_op | source)
XLA Modules:
  0.0 417.9 jit_solution(7296033910153623969)
XLA Ops:
  1.1 4.1 collective-permute-start.12
  10.1 7.5 %all-to-all-start = ((s32[32,1,2]{2,1,0:T(1,128)}), s32[32,1,2]{2,1,0:T(1,128)S(1)}, u32[]{:S(2)}, u32[]{:S(2)}) async-start(s32[32,1,2]{2,1,0:T(1,128)} %bitcast.2), calls=%async_computation | async-start | bytes 32768 | tf_op jit(solution)/shard_map/all_to_all | solution.py:249
  19.0 4.8 %all-to-all-done = s32[32,1,2]{2,1,0:T(1,128)S(1)} async-done(((s32[32,1,2]{2,1,0:T(1,128)}), s32[32,1,2]{2,1,0:T(1,128)S(1)}, u32[]{:S(2)}, u32[]{:S(2)}) %all-to-all-start) | async-done | bytes 288 | tf_op jit(solution)/shard_map/all_to_all | solution.py:249
  24.3 3.0 gather_fusion
  27.4 6.0 %all-to-all-start.1 = ((bf16[64,2,128,128]{3,2,1,0:T(8,128)(2,1)}), bf16[64,2,128,128]{3,2,1,0:T(8,128)(2,1)}, u32[]{:S(2)}, u32[]{:S(2)}) async-start(bf16[64,2,128,128]{3,2,1,0:T(8,128)(2,1)} %gather_fusion), calls=%async_computation.1 | async-start | bytes 8388608 | tf_op jit(solution)/shard_map/all_to_all | solution.py:293
  33.4 2.0 collective-permute-start.15
  35.5 2.3 collective-permute-start.14
  39.5 9.0 %collective-permute-done.15 = bf16[4,2,128,256]{3,2,1,0:T(8,128)(2,1)S(1)} collective-permute-done((bf16[4,2,128,256]{3,2,1,0:T(8,128)(2,1)S(1)}, bf16[4,2,128,256]{3,2,1,0:T(8,128)(2,1)S(1)}, u32[]{:S(2)}, u32[]{:S(2)}) %collective-permute-start.15) | collective-permute-done | bytes 524320 | tf_op jit(solution)/shard_map/ppermute | solution.py:283
  48.5 3.3 collective-permute-done.14
  51.8 10.1 %collective-permute-done.13 = bf16[4,2,128,256]{3,2,1,0:T(8,128)(2,1)S(1)} collective-permute-done((bf16[4,2,128,256]{3,2,1,0:T(8,128)(2,1)S(1)}, bf16[4,2,128,256]{3,2,1,0:T(8,128)(2,1)S(1)}, u32[]{:S(2)}, u32[]{:S(2)}) %collective-permute-start.13) | collective-permute-done | bytes 524320 | tf_op jit(solution)/shard_map/ppermute | solution.py:283
  62.2 5.4 %gather_fusion.2 = bf16[64,2,128,256]{3,2,1,0:T(8,128)(2,1)} fusion(bf16[16,2,128,256]{3,2,1,0:T(8,128)(2,1)S(1)} %pad_maximum_fusion.1, s32[1024]{0:T(1024)S(1)} %pad_clamp_fusion), kind=kCustom, calls=%fused_computation.2 | custom fusion | bytes 16777472 | tf_op jit(solution)/shard_map/gather | solution.py:293
  67.6 16.8 %all-to-all-done.1.block_ref = bf16[64,2,128,128]{3,2,1,0:T(8,128)(2,1)} async-done(((bf16[64,2,128,128]{3,2,1,0:T(8,128)(2,1)}), bf16[64,2,128,128]{3,2,1,0:T(8,128)(2,1)}, u32[]{:S(2)}, u32[]{:S(2)}) %all-to-all-start.1) | async-done | bytes 4194336 | tf_op jit(solution)/shard_map/all_to_all | solution.py:293
  84.4 7.9 %all-to-all-start.3 = ((bf16[64,2,128,256]{3,2,1,0:T(8,128)(2,1)}), bf16[64,2,128,256]{3,2,1,0:T(8,128)(2,1)}, u32[]{:S(2)}, u32[]{:S(2)}) async-start(bf16[64,2,128,256]{3,2,1,0:T(8,128)(2,1)} %gather_fusion.2), calls=%async_computation.3 | async-start | bytes 16777216 | tf_op jit(solution)/shard_map/all_to_all | solution.py:293
  97.9 111.1 %collective-permute-done.5 = bf16[2,512,512]{2,1,0:T(8,128)(2,1)} collective-permute-done((bf16[2,512,512]{2,1,0:T(8,128)(2,1)}, bf16[2,512,512]{2,1,0:T(8,128)(2,1)}, u32[]{:S(2)}, u32[]{:S(2)}) %collective-permute-start.5) | collective-permute-done | bytes 1048608 | tf_op jit(solution)/shard_map/ppermute | solution.py:263
  210.8 4.2 %collective-permute-done.7.rest_3_ = bf16[2,512,512]{2,1,0:T(8,128)(2,1)} collective-permute-done((bf16[2,512,512]{2,1,0:T(8,128)(2,1)S(1)}, bf16[2,512,512]{2,1,0:T(8,128)(2,1)}, u32[]{:S(2)}, u32[]{:S(2)}) %collective-permute-start.7) | collective-permute-done | bytes 1048608 | tf_op jit(solution)/shard_map/ppermute | solution.py:263
  215.0 27.5 %collective-permute-done.6.rest_2_ = bf16[2,512,512]{2,1,0:T(8,128)(2,1)} collective-permute-done((bf16[2,512,512]{2,1,0:T(8,128)(2,1)}, bf16[2,512,512]{2,1,0:T(8,128)(2,1)}, u32[]{:S(2)}, u32[]{:S(2)}) %collective-permute-start.6) | collective-permute-done | bytes 1048608 | tf_op jit(solution)/shard_map/ppermute | solution.py:263
  244.0 2.0 pad_maximum_fusion
  247.3 2.0 collective-permute-start.2
  249.3 2.3 collective-permute-start.1
  251.9 13.8 %collective-permute-done.9.rest_4_ = bf16[2,512,512]{2,1,0:T(8,128)(2,1)S(1)} collective-permute-done((bf16[2,512,512]{2,1,0:T(8,128)(2,1)S(1)}, bf16[2,512,512]{2,1,0:T(8,128)(2,1)S(1)}, u32[]{:S(2)}, u32[]{:S(2)}) %collective-permute-start.9) | collective-permute-done | bytes 1048608 | tf_op jit(solution)/shard_map/ppermute | solution.py:263
  266.7 32.7 %shard_map.64.state_ref = f32[2,4,640,384]{3,2,1,0:T(8,128)} custom-call(s32[1]{0:T(128)} %bitcast.place_ref, bf16[512,2560]{1,0:T(8,128)(2,1)} %q_ref.11, bf16[2,512,512]{2,1,0:T(8,128)(2,1)} %bitcast.32, bf16[3,2,512,512]{3,2,1,0:T(8,128)(2,1)} %collective-permute-done.8.rest_0_, bf16[2,512,512]{2,1,0:T(8,128)(2,1)} %copy-done.5, ...), custom_call_target="tpu_custom_call" | custom-call | flops 10737418240 | bytes 13369344 | tf_op jit(solution)/shard_map/pallas_call | solution.py:132
  299.3 32.8 %shard_map.65.state_ref = f32[2,4,640,384]{3,2,1,0:T(8,128)} custom-call(s32[1]{0:T(128)} %bitcast.place_ref, bf16[512,2560]{1,0:T(8,128)(2,1)} %q_ref.11, bf16[2,512,512]{2,1,0:T(8,128)(2,1)} %bitcast.33, bf16[3,2,512,512]{3,2,1,0:T(8,128)(2,1)} %collective-permute-done.8.rest_0_, bf16[2,512,512]{2,1,0:T(8,128)(2,1)} %copy-done.5, ...), custom_call_target="tpu_custom_call" | custom-call | flops 10737418240 | bytes 13369344 | tf_op jit(solution)/shard_map/pallas_call | solution.py:132
  332.1 8.7 %shard_map.66.rest_0_ = bf16[512,2560]{1,0:T(8,128)(2,1)} custom-call(s32[4]{0:T(128)S(1)} %copy-done.3, s32[4,8]{1,0:T(4,128)S(1)} %fusion.6.pos_ref, bf16[512,2560]{1,0:T(8,128)(2,1)S(1)} %copy-done, f32[2,4,640,384]{3,2,1,0:T(8,128)} %shard_map.64.state_ref, bf16[64,2,128,128]{3,2,1,0:T(8,128)(2,1)} %all-to-all-done.1.block_ref), custom_call_target="tpu_custom_call" | custom-call | flops 1342177280 | bytes 9437184 | tf_op jit(solution)/shard_map/pallas_call | solution.py:210
  340.9 2.3 pad_maximum_fusion.3
  343.1 4.3 %gather_fusion.1 = bf16[64,2,128,128]{3,2,1,0:T(8,128)(2,1)} fusion(bf16[16,2,128,128]{3,2,1,0:T(8,128)(2,1)} %pad_maximum_fusion.3, s32[1024]{0:T(1024)S(1)} %pad_clamp_fusion), kind=kCustom, calls=%fused_computation.1 | custom fusion | bytes 8388864 | tf_op jit(solution)/shard_map/gather | solution.py:293
  347.4 11.0 %all-to-all-start.2 = ((bf16[64,2,128,128]{3,2,1,0:T(8,128)(2,1)}), bf16[64,2,128,128]{3,2,1,0:T(8,128)(2,1)}, u32[]{:S(2)}, u32[]{:S(2)}) async-start(bf16[64,2,128,128]{3,2,1,0:T(8,128)(2,1)} %gather_fusion.1), calls=%async_computation.2 | async-start | bytes 8388608 | tf_op jit(solution)/shard_map/all_to_all | solution.py:293
  358.4 3.2 copy-done.2
  361.7 7.5 %shard_map.67.rest_0_ = bf16[512,2560]{1,0:T(8,128)(2,1)} custom-call(s32[4]{0:T(128)S(1)} %copy-done.3, s32[4,8]{1,0:T(4,128)S(1)} %fusion.6.pos_ref, bf16[512,2560]{1,0:T(8,128)(2,1)S(1)} %copy-done, f32[2,4,640,384]{3,2,1,0:T(8,128)S(1)} %copy-done.2, bf16[64,2,128,256]{3,2,1,0:T(8,128)(2,1)} %all-to-all-done.3.block_ref, ...), custom_call_target="tpu_custom_call", output_to_operand_aliasing={{}: (5, {})} | custom-call | flops 1342177280 | bytes 13631488 | tf_op jit(solution)/shard_map/pallas_call | solution.py:210
  369.2 3.2 copy-done.1
  372.4 7.5 %shard_map.68.rest_0_ = bf16[512,2560]{1,0:T(8,128)(2,1)} custom-call(s32[4]{0:T(128)S(1)} %copy-done.3, s32[4,8]{1,0:T(4,128)S(1)} %fusion.6.pos_ref, bf16[512,2560]{1,0:T(8,128)(2,1)S(1)} %copy-done, f32[2,4,640,384]{3,2,1,0:T(8,128)S(1)} %copy-done.1, bf16[64,2,128,256]{3,2,1,0:T(8,128)(2,1)} %all-to-all-done.3.block_ref, ...), custom_call_target="tpu_custom_call", output_to_operand_aliasing={{}: (5, {})} | custom-call | flops 1342177280 | bytes 13631488 | tf_op jit(solution)/shard_map/pallas_call | solution.py:210
  379.9 29.3 %all-to-all-done.2.block_ref = bf16[64,2,128,128]{3,2,1,0:T(8,128)(2,1)} async-done(((bf16[64,2,128,128]{3,2,1,0:T(8,128)(2,1)}), bf16[64,2,128,128]{3,2,1,0:T(8,128)(2,1)}, u32[]{:S(2)}, u32[]{:S(2)}) %all-to-all-start.2) | async-done | bytes 4194336 | tf_op jit(solution)/shard_map/all_to_all | solution.py:293
  409.2 8.7 %shard_map.69 = bf16[512,2560]{1,0:T(8,128)(2,1)} custom-call(s32[4]{0:T(128)S(1)} %copy-done.3, s32[4,8]{1,0:T(4,128)S(1)} %fusion.6.pos_ref, bf16[512,2560]{1,0:T(8,128)(2,1)S(1)} %copy-done, f32[2,4,640,384]{3,2,1,0:T(8,128)} %shard_map.65.state_ref, bf16[64,2,128,128]{3,2,1,0:T(8,128)(2,1)} %all-to-all-done.2.block_ref, ...), custom_call_target="tpu_custom_call", output_to_operand_aliasing={{}: (5, {})} | custom-call | flops 1342177280 | bytes 9437184 | tf_op jit(solution)/shard_map/pallas_call | solution.py:210
  (63 shorter events, 21.0 us)
Async XLA Ops:
  1.1 23.1 %collective-permute-start.12 = (bf16[4,2,128,128]{3,2,1,0:T(8,128)(2,1)S(1)}, bf16[4,2,128,128]{3,2,1,0:T(8,128)(2,1)S(1)}, u32[]{:S(2)}, u32[]{:S(2)}) collective-permute-start(bf16[4,2,128,128]{3,2,1,0:T(8,128)(2,1)S(1)} %get-tuple-element.35), channel_id=1, source_target_pairs={{0,96},{32,0},{64,32},{96,64},{1,97},{33,1},{65,33},{97,65},{2,98}... | collective-permute-start | bytes 786440 | tf_op jit(solution)/shard_map/ppermute | solution.py:283
  5.2 19.0 %collective-permute-start.11 = (bf16[4,2,128,128]{3,2,1,0:T(8,128)(2,1)S(1)}, bf16[4,2,128,128]{3,2,1,0:T(8,128)(2,1)S(1)}, u32[]{:S(2)}, u32[]{:S(2)}) collective-permute-start(bf16[4,2,128,128]{3,2,1,0:T(8,128)(2,1)S(1)} %get-tuple-element.35), channel_id=1, source_target_pairs={{0,64},{32,96},{64,0},{96,32},{1,65},{33,97},{65,1},{97,33},{2,66}... | collective-permute-start | bytes 786440 | tf_op jit(solution)/shard_map/ppermute | solution.py:283
  5.2 19.0 %collective-permute-start.10 = (bf16[4,2,128,128]{3,2,1,0:T(8,128)(2,1)S(1)}, bf16[4,2,128,128]{3,2,1,0:T(8,128)(2,1)S(1)}, u32[]{:S(2)}, u32[]{:S(2)}) collective-permute-start(bf16[4,2,128,128]{3,2,1,0:T(8,128)(2,1)S(1)} %get-tuple-element.35), channel_id=1, source_target_pairs={{0,32},{32,64},{64,96},{96,0},{1,33},{33,65},{65,97},{97,1},{2,34}... | collective-permute-start | bytes 786440 | tf_op jit(solution)/shard_map/ppermute | solution.py:283
  10.1 13.7 %all-to-all-start = ((s32[32,1,2]{2,1,0:T(1,128)}), s32[32,1,2]{2,1,0:T(1,128)S(1)}, u32[]{:S(2)}, u32[]{:S(2)}) async-start(s32[32,1,2]{2,1,0:T(1,128)} %bitcast.2), calls=%async_computation | async-start | bytes 32768 | tf_op jit(solution)/shard_map/all_to_all | solution.py:249
  19.0 226.9 %copy-start.4 = (bf16[512,2,512]{2,0,1:T(8,128)(2,1)}, bf16[512,2,512]{2,0,1:T(8,128)(2,1)S(1)}, u32[]{:S(2)}) copy-start(bf16[512,2,512]{2,0,1:T(8,128)(2,1)S(1)} %copy.25) | copy-start | bytes 3145732
  27.4 6.0 %copy-start.6 = (bf16[4,2,128,512]{3,2,1,0:T(8,128)(2,1)S(1)}, bf16[4,2,128,512]{3,2,1,0:T(8,128)(2,1)}, u32[]{:S(2)}) copy-start(bf16[4,2,128,512]{3,2,1,0:T(8,128)(2,1)} %param.8) | copy-start | bytes 3145732
  27.4 57.0 %all-to-all-start.1 = ((bf16[64,2,128,128]{3,2,1,0:T(8,128)(2,1)}), bf16[64,2,128,128]{3,2,1,0:T(8,128)(2,1)}, u32[]{:S(2)}, u32[]{:S(2)}) async-start(bf16[64,2,128,128]{3,2,1,0:T(8,128)(2,1)} %gather_fusion), calls=%async_computation.1 | async-start | bytes 8388608 | tf_op jit(solution)/shard_map/all_to_all | solution.py:293
  33.4 15.1 %collective-permute-start.15 = (bf16[4,2,128,256]{3,2,1,0:T(8,128)(2,1)S(1)}, bf16[4,2,128,256]{3,2,1,0:T(8,128)(2,1)S(1)}, u32[]{:S(2)}, u32[]{:S(2)}) collective-permute-start(bf16[4,2,128,256]{3,2,1,0:T(8,128)(2,1)S(1)} %slice.11), channel_id=1, source_target_pairs={{0,96},{32,0},{64,32},{96,64},{1,97},{33,1},{65,33},{97,65},{2,98}... | collective-permute-start | bytes 1572872 | tf_op jit(solution)/shard_map/ppermute | solution.py:283
  35.5 16.3 %collective-permute-start.14 = (bf16[4,2,128,256]{3,2,1,0:T(8,128)(2,1)S(1)}, bf16[4,2,128,256]{3,2,1,0:T(8,128)(2,1)S(1)}, u32[]{:S(2)}, u32[]{:S(2)}) collective-permute-start(bf16[4,2,128,256]{3,2,1,0:T(8,128)(2,1)S(1)} %slice.11), channel_id=1, source_target_pairs={{0,64},{32,96},{64,0},{96,32},{1,65},{33,97},{65,1},{97,33},{2,66}... | collective-permute-start | bytes 1572872 | tf_op jit(solution)/shard_map/ppermute | solution.py:283
  37.8 24.1 %collective-permute-start.13 = (bf16[4,2,128,256]{3,2,1,0:T(8,128)(2,1)S(1)}, bf16[4,2,128,256]{3,2,1,0:T(8,128)(2,1)S(1)}, u32[]{:S(2)}, u32[]{:S(2)}) collective-permute-start(bf16[4,2,128,256]{3,2,1,0:T(8,128)(2,1)S(1)} %slice.11), channel_id=1, source_target_pairs={{0,32},{32,64},{64,96},{96,0},{1,33},{33,65},{65,97},{97,1},{2,34}... | collective-permute-start | bytes 1572872 | tf_op jit(solution)/shard_map/ppermute | solution.py:283
  37.8 56.2 %collective-permute-start.4 = (bf16[2,512,512]{2,1,0:T(8,128)(2,1)S(1)}, bf16[2,512,512]{2,1,0:T(8,128)(2,1)}, u32[]{:S(2)}, u32[]{:S(2)}) collective-permute-start(bf16[2,512,512]{2,1,0:T(8,128)(2,1)S(1)} %bitcast.27), channel_id=1, source_target_pairs={{6,14},{7,15},{14,22},{15,23},{22,30},{23,31},{30,38},{31,39},{38,... | collective-permute-start | bytes 3145736 | tf_op jit(solution)/shard_map/ppermute | solution.py:263
  84.4 263.0 %all-to-all-start.3 = ((bf16[64,2,128,256]{3,2,1,0:T(8,128)(2,1)}), bf16[64,2,128,256]{3,2,1,0:T(8,128)(2,1)}, u32[]{:S(2)}, u32[]{:S(2)}) async-start(bf16[64,2,128,256]{3,2,1,0:T(8,128)(2,1)} %gather_fusion.2), calls=%async_computation.3 | async-start | bytes 16777216 | tf_op jit(solution)/shard_map/all_to_all | solution.py:293
  92.3 4.3 %collective-permute-start.3 = (bf16[2,512,512]{2,1,0:T(8,128)(2,1)S(1)}, bf16[2,512,512]{2,1,0:T(8,128)(2,1)}, u32[]{:S(2)}, u32[]{:S(2)}) collective-permute-start(bf16[2,512,512]{2,1,0:T(8,128)(2,1)S(1)} %bitcast.28), channel_id=1, source_target_pairs={{1,3},{2,4},{3,5},{4,6},{5,7},{9,11},{10,12},{11,13},{12,14},{13,1... | collective-permute-start | bytes 3145736 | tf_op jit(solution)/shard_map/ppermute | solution.py:263
  94.0 115.0 %collective-permute-start.5 = (bf16[2,512,512]{2,1,0:T(8,128)(2,1)}, bf16[2,512,512]{2,1,0:T(8,128)(2,1)}, u32[]{:S(2)}, u32[]{:S(2)}) collective-permute-start(bf16[2,512,512]{2,1,0:T(8,128)(2,1)} %collective-permute-done.4), channel_id=1, source_target_pairs={{6,0},{7,1},{14,8},{15,9},{22,16},{23,17},{30,24},{31,25},{38,32},... | collective-permute-start | bytes 3145736 | tf_op jit(solution)/shard_map/ppermute | solution.py:263
  95.3 119.7 %collective-permute-start.7 = (bf16[2,512,512]{2,1,0:T(8,128)(2,1)S(1)}, bf16[2,512,512]{2,1,0:T(8,128)(2,1)}, u32[]{:S(2)}, u32[]{:S(2)}) collective-permute-start(bf16[2,512,512]{2,1,0:T(8,128)(2,1)S(1)} %bitcast.29), channel_id=1, source_target_pairs={{1,7},{2,8},{3,9},{9,15},{10,16},{11,17},{17,23},{18,24},{19,25},{... | collective-permute-start | bytes 3145736 | tf_op jit(solution)/shard_map/ppermute | solution.py:263
  96.6 145.9 %collective-permute-start.6 = (bf16[2,512,512]{2,1,0:T(8,128)(2,1)}, bf16[2,512,512]{2,1,0:T(8,128)(2,1)}, u32[]{:S(2)}, u32[]{:S(2)}) collective-permute-start(bf16[2,512,512]{2,1,0:T(8,128)(2,1)} %collective-permute-done.3), channel_id=1, source_target_pairs={{3,5},{4,6},{5,7},{6,8},{7,9},{11,13},{12,14},{13,15},{14,16},{15,... | collective-permute-start | bytes 3145736 | tf_op jit(solution)/shard_map/ppermute | solution.py:263
  210.7 35.2 %copy-start.5 = (bf16[2,512,512]{2,1,0:T(8,128)(2,1)}, bf16[2,512,512]{2,1,0:T(8,128)(2,1)S(1)}, u32[]{:S(2)}) copy-start(bf16[2,512,512]{2,1,0:T(8,128)(2,1)S(1)} %get-tuple-element.32.rest_1_) | copy-start | bytes 3145732
  244.0 7.8 %copy-start.3 = (s32[4]{0:T(128)S(1)}, s32[4]{0:T(128)}, u32[]{:S(2)}) copy-start(s32[4]{0:T(128)} %count_ref.7) | copy-start | bytes 52
  246.0 19.7 %collective-permute-start.8 = (bf16[3,2,512,512]{3,2,1,0:T(8,128)(2,1)}, bf16[3,2,512,512]{3,2,1,0:T(8,128)(2,1)}, u32[]{:S(2)}, u32[]{:S(2)}) collective-permute-start(bf16[3,2,512,512]{3,2,1,0:T(8,128)(2,1)} %pad_maximum_fusion), channel_id=1, source_target_pairs={{0,1},{1,0},{2,3},{3,2},{4,5},{5,4},{6,7},{7,6},{8,9},{9,8},{10,11... | collective-permute-start | bytes 9437192 | tf_op jit(solution)/shard_map/ppermute | solution.py:275
  246.0 19.7 %collective-permute-start.9 = (bf16[2,512,512]{2,1,0:T(8,128)(2,1)S(1)}, bf16[2,512,512]{2,1,0:T(8,128)(2,1)S(1)}, u32[]{:S(2)}, u32[]{:S(2)}) collective-permute-start(bf16[2,512,512]{2,1,0:T(8,128)(2,1)S(1)} %bitcast.31), channel_id=1, source_target_pairs={{1,8},{9,16},{17,24},{25,32},{33,40},{41,48},{49,56},{57,64},{65,7... | collective-permute-start | bytes 3145736 | tf_op jit(solution)/shard_map/ppermute | solution.py:263
  247.3 93.6 %collective-permute-start.2 = (bf16[4,2,128,128]{3,2,1,0:T(8,128)(2,1)S(1)}, bf16[4,2,128,128]{3,2,1,0:T(8,128)(2,1)}, u32[]{:S(2)}, u32[]{:S(2)}) collective-permute-start(bf16[4,2,128,128]{3,2,1,0:T(8,128)(2,1)S(1)} %get-tuple-element.21), channel_id=1, source_target_pairs={{0,96},{32,0},{64,32},{96,64},{1,97},{33,1},{65,33},{97,65},{2,98}... | collective-permute-start | bytes 786440 | tf_op jit(solution)/shard_map/ppermute | solution.py:283
  249.3 91.5 %collective-permute-start.1 = (bf16[4,2,128,128]{3,2,1,0:T(8,128)(2,1)S(1)}, bf16[4,2,128,128]{3,2,1,0:T(8,128)(2,1)}, u32[]{:S(2)}, u32[]{:S(2)}) collective-permute-start(bf16[4,2,128,128]{3,2,1,0:T(8,128)(2,1)S(1)} %get-tuple-element.21), channel_id=1, source_target_pairs={{0,64},{32,96},{64,0},{96,32},{1,65},{33,97},{65,1},{97,33},{2,66}... | collective-permute-start | bytes 786440 | tf_op jit(solution)/shard_map/ppermute | solution.py:283
  251.6 89.2 %collective-permute-start = (bf16[4,2,128,128]{3,2,1,0:T(8,128)(2,1)S(1)}, bf16[4,2,128,128]{3,2,1,0:T(8,128)(2,1)}, u32[]{:S(2)}, u32[]{:S(2)}) collective-permute-start(bf16[4,2,128,128]{3,2,1,0:T(8,128)(2,1)S(1)} %get-tuple-element.21), channel_id=1, source_target_pairs={{0,32},{32,64},{64,96},{96,0},{1,33},{33,65},{65,97},{97,1},{2,34}... | collective-permute-start | bytes 786440 | tf_op jit(solution)/shard_map/ppermute | solution.py:283
  265.7 1.0 copy-start.7
  299.3 32.8 %copy-start = (bf16[512,2560]{1,0:T(8,128)(2,1)S(1)}, bf16[512,2560]{1,0:T(8,128)(2,1)}, u32[]{:S(2)}) copy-start(bf16[512,2560]{1,0:T(8,128)(2,1)} %q_ref.11) | copy-start | bytes 7864324
  347.4 61.8 %all-to-all-start.2 = ((bf16[64,2,128,128]{3,2,1,0:T(8,128)(2,1)}), bf16[64,2,128,128]{3,2,1,0:T(8,128)(2,1)}, u32[]{:S(2)}, u32[]{:S(2)}) async-start(bf16[64,2,128,128]{3,2,1,0:T(8,128)(2,1)} %gather_fusion.1), calls=%async_computation.2 | async-start | bytes 8388608 | tf_op jit(solution)/shard_map/all_to_all | solution.py:293
  358.4 3.2 copy-start.2
  369.2 3.2 copy-start.1
